TPU v7x, 256 devices: a whole 4x4x8 slice. The times are simulated.
256 devices in a mesh: row: 16 (over x_hi, y, core), col: 16 (over z, x_lo).
Axes of the slice: x: 4 (x_hi: 2, x_lo: 2; x = x_hi * 2 + x_lo), y: 4, z: 8, core: 2. Of those that a mesh axis runs over, the one named last changes fastest.
Arguments:
- vectors: float32 [16, 32768], P(None, ('col', 'row')), may hold values from -6 to 6
- tile_blocks: float32 [16, 16, 128, 128, 128], P('row', 'col'), may hold values from -0.046875 to 0.046875
- coords: int32 [16, 16, 128], P('row', 'col'), may hold values from 0 to 255, as said below
- counts: int32 [16, 16], P('row', 'col'), may hold values from 1 to 128, as said below
Outputs:
- product: float32 [16, 32768], P(None, ('col', 'row'))
Inputs may be any that keep to these rules, and one draw needn't show every extreme that they name: `counts`: every cell has at least one live slot and some cell has exactly 128. `coords`: within one cell all 128 entries are distinct; slots at or past counts hold no tile of S.
All inputs are finite; a program needn't handle non-finite values.
Results may differ from a plain program's by a relative error of at most 0.0003.
Values sent between devices are 32-bit elements; how exact they have to be, the bound alone decides.
No kernel may reach another device: no remote copies, remote signals or barrier semaphores. Data moves between devices by JAX's collectives and lax.ppermute only.
A program may use at most 64 MiB of HBM per device.

v0:
```python
import jax
import jax.numpy as jnp
from jax import lax
from jax.sharding import PartitionSpec as P

HIGH = lax.Precision.HIGHEST


def from_root(value, axis, source):
    kept = jnp.where(lax.axis_index(axis) == source, value, 0).astype(value.dtype)
    return lax.psum(kept, axis)


def slot_terms(blocks, slot_coords, live_mask, x_col, x_row):
    vec_count = x_col.shape[0]
    tile_size = blocks.shape[-1]
    seg_tiles = x_row.shape[1] // tile_size
    col_tiles = x_col.shape[1] // tile_size
    row_pos = slot_coords // col_tiles
    col_pos = slot_coords % col_tiles
    picked_col = jnp.take(x_col.reshape(vec_count, col_tiles, tile_size), col_pos, axis=1)
    picked_row = jnp.take(x_row.reshape(vec_count, seg_tiles, tile_size), row_pos, axis=1)
    normal = jnp.einsum("vsk,smk->vsm", picked_col, blocks, precision=HIGH)
    transposed = jnp.einsum("vsm,smk->vsk", picked_row, blocks, precision=HIGH)
    onehot_rows = (row_pos[:, None] == jnp.arange(seg_tiles, dtype=jnp.int32)[None, :]).astype(
        jnp.float32
    ) * live_mask[:, None]
    onehot_cols = (col_pos[:, None] == jnp.arange(col_tiles, dtype=jnp.int32)[None, :]).astype(
        jnp.float32
    ) * live_mask[:, None]
    row_terms = jnp.einsum("st,vsm->vtm", onehot_rows, normal, precision=HIGH).reshape(
        vec_count, seg_tiles * tile_size
    )
    col_terms = jnp.einsum("st,vsk->vtk", onehot_cols, transposed, precision=HIGH).reshape(
        vec_count, col_tiles * tile_size
    )
    return (row_terms, col_terms)


def local(vectors, tile_blocks, coords, counts):
    n_row = lax.axis_size("row")
    n_col = lax.axis_size("col")
    seg_ratio = n_row // n_col
    max_slots = tile_blocks.shape[2]
    tile_size = tile_blocks.shape[-1]
    blocks = tile_blocks.reshape(max_slots, tile_size, tile_size)
    slot_coords = coords.reshape(max_slots)
    slot_count = counts.reshape(())
    row_idx = lax.axis_index("row")
    col_idx = lax.axis_index("col")
    x_col = lax.all_gather(vectors, "row", axis=1, tiled=True)
    x_row = from_root(x_col, "col", row_idx // seg_ratio)
    live_mask = (jnp.arange(max_slots, dtype=jnp.int32) < slot_count).astype(jnp.float32)
    row_terms, col_terms = slot_terms(blocks, slot_coords, live_mask, x_col, x_row)
    whole_row = lax.psum(row_terms, "col")
    is_owner = (col_idx == row_idx // seg_ratio).astype(jnp.float32)
    placed = whole_row * is_owner
    return lax.psum_scatter(col_terms + placed, "row", scatter_dimension=1, tiled=True)


def solution(mesh):
    return jax.shard_map(
        local,
        mesh=mesh,
        in_specs=(
            P(None, ("col", "row")),
            P("row", "col", None, None, None),
            P("row", "col", None),
            P("row", "col"),
        ),
        out_specs=P(None, ("col", "row")),
        check_vma=False,
    )
```

profile of v0, /device:TPU:1, one launch (start us, length us, event | category | flops | bytes accessed | tf_op | source)
XLA Modules:
  0.0 275.0 jit_solution(18044098846579297185)
XLA Ops:
  6.5 0.0 all-reduce.3.cloned.1.call-start
  7.2 0.7 compare_and_fusion.1
  7.9 26.3 %all_gather.3 = f32[16,2048]{1,0:T(8,128)S(1)} all-gather(f32[16,128]{1,0:T(8,128)} %param.6), channel_id=1, replica_groups=mesh['row'=16,'col'=16] {'row'}, dimensions={1}, use_global_device_ids=true | all-gather | bytes 139264 | tf_op jit(solution)/shard_map/all_gather | solution.py:51
  34.2 0.8 gather_fusion.1
  35.0 15.5 %fusion.7 = f32[16,128,128]{2,0,1:T(8,128)S(1)} fusion(f32[1,1,128,128,128]{4,3,2,1,0:T(8,128)} %param.7, f32[128,16,128]{2,1,0:T(8,128)S(1)} %gather_fusion.1, pred[128]{0:T(512)(128)(4,1)S(1)} %get-tuple-element.12), kind=kOutput, calls=%fused_computation.7 | convolution fusion | flops 402915328 | bytes 10485888 | tf_op jit(solution)/shard_map/vsk,smk->vsm/dot_general | solution.py:23
  50.5 0.9 fusion.12
  51.4 0.7 copy.21
  52.1 0.7 copy_bitcast_fusion.2
  52.8 0.0 all-reduce.3.cloned.1.call-update
  52.8 0.0 reduce-scatter.2.cloned.1.call-start
  52.9 124.6 %all-reduce.3.cloned.1.call-done = (f32[16,16,128]{2,0,1:T(8,128)}, f32[16,2048]{1,0:T(8,128)}) async-done(((f32[16,16,128]{2,0,1:T(8,128)}, f32[16,2048]{1,0:T(8,128)}), (f32[16,16,128]{2,0,1:T(8,128)}, f32[16,2048]{1,0:T(8,128)})) %all-reduce.3.cloned.1.call-update) | async-done | bytes 262160 | tf_op jit(solution)/shard_map/psum | solution.py:11
  177.5 0.0 copy-start
  177.5 1.6 gather_fusion
  179.1 9.6 %fusion.4 = f32[16,128,128]{2,0,1:T(8,128)S(1)} fusion(f32[1,1,128,128,128]{4,3,2,1,0:T(8,128)} %param.7, f32[128,16,128]{2,1,0:T(8,128)S(1)} %gather_fusion, pred[128]{0:T(512)(128)(4,1)S(1)} %get-tuple-element.8), kind=kOutput, calls=%fused_computation.6 | convolution fusion | flops 402915328 | bytes 10485888 | tf_op jit(solution)/shard_map/vsm,smk->vsk/dot_general | solution.py:24
  188.7 0.9 fusion.14
  189.6 0.0 copy-done
  189.6 0.7 bitcast_add_fusion
  190.3 0.0 reduce-scatter.2.cloned.1.call-update
  190.3 77.9 %reduce-scatter.2.cloned.1.call-done = f32[16,128]{1,0:T(8,128)} async-done(((f32[16,2048]{1,0:T(8,128)}), f32[16,128]{1,0:T(8,128)}) %reduce-scatter.2.cloned.1.call-update) | async-done | bytes 8208 | tf_op jit(solution)/shard_map/reduce_scatter | solution.py:58
  (5 shorter events, 0.0 us)
Async XLA Ops:
  6.5 170.9 %all-reduce.3.cloned.1.call-start = ((), (), s32[]{:S(2)}) async-start(), calls=%async_computation.2 | async-start | bytes 524288 | tf_op jit(solution)/shard_map/psum | solution.py:11
  52.8 215.4 %reduce-scatter.2.cloned.1.call-start = ((), (), s32[]{:S(2)}) async-start(), calls=%async_computation.1 | async-start | bytes 139264 | tf_op jit(solution)/shard_map/reduce_scatter | solution.py:58
  177.5 12.1 %copy-start = (f32[16,2048]{1,0:T(8,128)S(1)}, f32[16,2048]{1,0:T(8,128)}, u32[]{:S(2)}) copy-start(f32[16,2048]{1,0:T(8,128)} %get-tuple-element.7) | copy-start | bytes 393220
Sparse Core Ops, SparseCore 0:
  52.9 124.5 all-reduce.2
  190.5 77.6 reduce-scatter.1
where the time goes:
time: 276 us; the launch traced here: 275 us
  waiting for transfers between devices  202 us (73%)
  matrix products  26.9 us (10%)
  blocking collectives  26.3 us (10%)
  between operations  14.1 us (5%)
  local copies, waits for them, and re-layouts  3.07 us (1%)
    psum x1, waiting for transfers between devices, from_root(): return lax.psum(kept, axis)  125 us
    reduce_scatter x1, waiting for transfers between devices, local(): lax.psum_scatter(col_terms + placed, 'row', scatter_dimension=1, tiled=True)  77.9 us
    all_gather x1, blocking collectives, local(): x_col = lax.all_gather(vectors, 'row', axis=1, tiled=True)  26.3 us
    dot_general x1, matrix products, slot_terms(): normal = jnp.einsum('vsk,smk->vsm', picked_col, blocks, precision=HIGH)  15.5 us
    dot_general x1, matrix products, slot_terms(): transposed = jnp.einsum('vsm,smk->vsk', picked_row, blocks, precision=HIGH)  9.6 us
  transfers between devices with their start and end apart: 2, of which 2 were waited for; matrix products, arithmetic and copies ran while one was open for 0% of the time, Pallas kernels for 0%

commit v1 on v0

v1 whole, which is shorter than its diff:
```python
import jax
import jax.numpy as jnp
from jax import lax
from jax.sharding import PartitionSpec as P

HIGH = lax.Precision.HIGHEST


def local(vectors, tile_blocks, coords, counts):
    n_row = lax.axis_size("row")
    n_col = lax.axis_size("col")
    max_slots = tile_blocks.shape[2]
    tile = tile_blocks.shape[-1]
    vecs = vectors.shape[0]
    flip = [(r * n_col + c, c * n_col + r) for r in range(n_row) for c in range(n_col)]
    blocks = tile_blocks.reshape(max_slots, tile, tile)
    pos = coords.reshape(max_slots)
    live = (jnp.arange(max_slots, dtype=jnp.int32) < counts.reshape(())).astype(jnp.float32)
    row_pos = pos // n_row
    col_pos = pos % n_row
    tiles = jnp.arange(n_row, dtype=jnp.int32)
    pick_row = (row_pos[:, None] == tiles[None, :]).astype(jnp.float32) * live[:, None]
    pick_col = (col_pos[:, None] == tiles[None, :]).astype(jnp.float32) * live[:, None]

    spread = jnp.broadcast_to(vectors[None], (n_row, vecs, tile))
    x_col = lax.all_to_all(spread, "row", 0, 0, tiled=True)
    x_row = lax.ppermute(x_col, ("row", "col"), flip)
    normal = jnp.einsum("svk,smk->svm", jnp.take(x_col, col_pos, axis=0), blocks, precision=HIGH)
    row_terms = jnp.einsum("st,svm->tvm", pick_row, normal, precision=HIGH)
    flipped = lax.ppermute(row_terms, ("row", "col"), flip)
    turned = jnp.einsum("svm,smk->svk", jnp.take(x_row, row_pos, axis=0), blocks, precision=HIGH)
    col_terms = jnp.einsum("st,svk->tvk", pick_col, turned, precision=HIGH)
    parts = lax.all_to_all(col_terms + flipped, "row", 0, 0, tiled=True)
    return jnp.sum(parts, axis=0)


def solution(mesh):
    return jax.shard_map(
        local,
        mesh=mesh,
        in_specs=(
            P(None, ("col", "row")),
            P("row", "col", None, None, None),
            P("row", "col", None),
            P("row", "col"),
        ),
        out_specs=P(None, ("col", "row")),
        check_vma=False,
    )
```

time: 276 us -> 91.3 us (0.33)
  waiting for transfers between devices: 202 us -> 17.6 us
  starting transfers between devices: 0.04 us -> 14 us
  between operations: 14.1 us -> 0.76 us
    psum x1 -> x0, waiting for transfers between devices: 125 us -> none  [from_root(): return lax.psum(kept, axis)]
    reduce_scatter x1 -> x0, waiting for transfers between devices: 77.9 us -> none  [local(): lax.psum_scatter(col_terms + placed, 'row', scatter_dimension=1, tiled=True)]
    all_to_all x0 -> x1, blocking collectives: none -> 27.6 us  [local(): parts = lax.all_to_all(col_terms + flipped, 'row', 0, 0, tiled=True)]
    all_gather x1 -> x0, blocking collectives: 26.3 us -> none  [local(): x_col = lax.all_gather(vectors, 'row', axis=1, tiled=True)]
    ppermute x0 -> x2, waiting for transfers between devices: none -> 11.3 us  [the longest x1 11.3 us: local(): flipped = lax.ppermute(row_terms, ('row', 'col'), flip)]
    all_to_all x0 -> x1, starting transfers between devices: none -> 8.44 us  [local(): x_col = lax.all_to_all(spread, 'row', 0, 0, tiled=True)]
    all_to_all x0 -> x1, waiting for transfers between devices: none -> 6.24 us  [local(): x_col = lax.all_to_all(spread, 'row', 0, 0, tiled=True)]
    ppermute x0 -> x2, starting transfers between devices: none -> 5.56 us  [the longest x1 2.79 us: local(): flipped = lax.ppermute(row_terms, ('row', 'col'), flip)]
  transfers between devices with their start and end apart: 2 -> 3, of which waited for: 2 -> 2; matrix products, arithmetic and copies ran while one was open for 0% -> 13% of each run, Pallas kernels for 0% -> 0%
where the time goes in v1:
time: 91.3 us; the launch traced here: 91 us
  blocking collectives  27.6 us (30%)
  matrix products  26.8 us (29%)
  waiting for transfers between devices  17.6 us (19%)
  starting transfers between devices  14 us (15%)
  local copies, waits for them, and re-layouts  2.91 us (3%)
  other arithmetic  1.31 us (1%)
    all_to_all x1, blocking collectives, local(): parts = lax.all_to_all(col_terms + flipped, 'row', 0, 0, tiled=True)  27.6 us
    dot_general x1, matrix products, local(): jnp.einsum('svk,smk->svm', jnp.take(x_col, col_pos, axis=0), blocks, prec...  15.5 us
    ppermute x1, waiting for transfers between devices, local(): flipped = lax.ppermute(row_terms, ('row', 'col'), flip)  11.3 us
    dot_general x1, matrix products, local(): jnp.einsum('svm,smk->svk', jnp.take(x_row, row_pos, axis=0), blocks, prec...  9.61 us
    all_to_all x1, starting transfers between devices, local(): x_col = lax.all_to_all(spread, 'row', 0, 0, tiled=True)  8.44 us
    all_to_all x1, waiting for transfers between devices, local(): x_col = lax.all_to_all(spread, 'row', 0, 0, tiled=True)  6.24 us
    ppermute x1, starting transfers between devices, local(): flipped = lax.ppermute(row_terms, ('row', 'col'), flip)  2.79 us
    ppermute x1, starting transfers between devices, local(): x_row = lax.ppermute(x_col, ('row', 'col'), flip)  2.76 us
  transfers between devices with their start and end apart: 3, of which 2 were waited for; matrix products, arithmetic and copies ran while one was open for 13% of the time, Pallas kernels for 0%

profile of v1, /device:TPU:1, one launch (start us, length us, event | category | flops | bytes accessed | tf_op | source)
XLA Modules:
  0.0 91.0 jit_solution(1260847767135247044)
XLA Ops:
  0.0 1.4 %broadcast_in_dim.8 = f32[16,16,128]{2,1,0:T(8,128)} broadcast(f32[16,128]{1,0:T(8,128)} %param.6), dimensions={1,2} | broadcast | bytes 139264 | tf_op jit(solution)/shard_map/broadcast_in_dim | solution.py:25
  1.4 8.4 %all-to-all-start = ((f32[16,16,128]{2,1,0:T(8,128)}), f32[16,16,128]{2,1,0:T(8,128)S(1)}, u32[]{:S(2)}, u32[]{:S(2)}) async-start(f32[16,16,128]{2,1,0:T(8,128)} %broadcast_in_dim.8), calls=%async_computation | async-start | bytes 262144 | tf_op jit(solution)/shard_map/all_to_all | solution.py:26
  9.8 0.7 compare_and_fusion.1
  11.2 6.2 %all-to-all-done = f32[16,16,128]{2,1,0:T(8,128)S(1)} async-done(((f32[16,16,128]{2,1,0:T(8,128)}), f32[16,16,128]{2,1,0:T(8,128)S(1)}, u32[]{:S(2)}, u32[]{:S(2)}) %all-to-all-start) | async-done | bytes 131104 | tf_op jit(solution)/shard_map/all_to_all | solution.py:26
  17.4 0.8 gather_fusion.1
  18.2 15.5 %fusion = f32[128,16,128]{2,1,0:T(8,128)S(1)} fusion(f32[1,1,128,128,128]{4,3,2,1,0:T(8,128)} %param.7, f32[128,16,128]{2,1,0:T(8,128)S(1)} %gather_fusion.1, pred[128]{0:T(512)(128)(4,1)S(1)} %get-tuple-element.10), kind=kOutput, calls=%fused_computation.2 | convolution fusion | flops 402915328 | bytes 10485888 | tf_op jit(solution)/shard_map/svk,smk->svm/dot_general | solution.py:28
  33.6 2.8 %collective-permute-start = (f32[16,16,128]{2,1,0:T(8,128)S(1)}, f32[16,16,128]{2,1,0:T(8,128)S(1)}, u32[]{:S(2)}, u32[]{:S(2)}) collective-permute-start(f32[16,16,128]{2,1,0:T(8,128)S(1)} %all-to-all-done), channel_id=1, source_target_pairs={{0,0},{1,16},{2,32},{3,48},{4,64},{5,80},{6,96},{7,112},{8,128},{9... | collective-permute-start | bytes 393224 | tf_op jit(solution)/shard_map/ppermute | solution.py:27
  36.4 0.9 fusion.4
  37.3 2.8 %collective-permute-start.1 = (f32[16,16,128]{2,0,1:T(8,128)S(1)}, f32[16,16,128]{2,0,1:T(8,128)S(1)}, u32[]{:S(2)}, u32[]{:S(2)}) collective-permute-start(f32[16,16,128]{2,0,1:T(8,128)S(1)} %fusion.4), channel_id=1, source_target_pairs={{0,0},{1,16},{2,32},{3,48},{4,64},{5,80},{6,96},{7,112},{8,128},{9... | collective-permute-start | bytes 393224 | tf_op jit(solution)/shard_map/ppermute | solution.py:30
  40.1 0.0 collective-permute-done
  40.1 0.8 gather_fusion
  40.9 9.6 %fusion.2 = f32[128,16,128]{2,1,0:T(8,128)S(1)} fusion(f32[1,1,128,128,128]{4,3,2,1,0:T(8,128)} %param.7, f32[128,16,128]{2,1,0:T(8,128)S(1)} %gather_fusion, pred[128]{0:T(512)(128)(4,1)S(1)} %get-tuple-element.6), kind=kOutput, calls=%fused_computation.4 | convolution fusion | flops 402915328 | bytes 10485888 | tf_op jit(solution)/shard_map/svm,smk->svk/dot_general | solution.py:31
  50.5 11.3 %collective-permute-done.1 = f32[16,16,128]{2,0,1:T(8,128)S(1)} collective-permute-done((f32[16,16,128]{2,0,1:T(8,128)S(1)}, f32[16,16,128]{2,0,1:T(8,128)S(1)}, u32[]{:S(2)}, u32[]{:S(2)}) %collective-permute-start.1) | collective-permute-done | bytes 131104 | tf_op jit(solution)/shard_map/ppermute | solution.py:30
  61.8 0.9 convolution_add_fusion
  62.7 27.6 %all_to_all.10 = f32[16,16,128]{2,1,0:T(8,128)S(1)} all-to-all(f32[16,16,128]{2,1,0:T(8,128)S(1)} %copy.5), channel_id=1, replica_groups=mesh['row'=16,'col'=16] {'row'}, dimensions={0} | all-to-all | bytes 262144 | tf_op jit(solution)/shard_map/all_to_all | solution.py:33
  90.4 0.6 reduce_sum.9
  (6 shorter events, 0.1 us)
Async XLA Ops:
  1.4 16.1 %all-to-all-start = ((f32[16,16,128]{2,1,0:T(8,128)}), f32[16,16,128]{2,1,0:T(8,128)S(1)}, u32[]{:S(2)}, u32[]{:S(2)}) async-start(f32[16,16,128]{2,1,0:T(8,128)} %broadcast_in_dim.8), calls=%async_computation | async-start | bytes 262144 | tf_op jit(solution)/shard_map/all_to_all | solution.py:26
  33.6 6.4 %collective-permute-start = (f32[16,16,128]{2,1,0:T(8,128)S(1)}, f32[16,16,128]{2,1,0:T(8,128)S(1)}, u32[]{:S(2)}, u32[]{:S(2)}) collective-permute-start(f32[16,16,128]{2,1,0:T(8,128)S(1)} %all-to-all-done), channel_id=1, source_target_pairs={{0,0},{1,16},{2,32},{3,48},{4,64},{5,80},{6,96},{7,112},{8,128},{9... | collective-permute-start | bytes 393224 | tf_op jit(solution)/shard_map/ppermute | solution.py:27
  37.3 24.5 %collective-permute-start.1 = (f32[16,16,128]{2,0,1:T(8,128)S(1)}, f32[16,16,128]{2,0,1:T(8,128)S(1)}, u32[]{:S(2)}, u32[]{:S(2)}) collective-permute-start(f32[16,16,128]{2,0,1:T(8,128)S(1)} %fusion.4), channel_id=1, source_target_pairs={{0,0},{1,16},{2,32},{3,48},{4,64},{5,80},{6,96},{7,112},{8,128},{9... | collective-permute-start | bytes 393224 | tf_op jit(solution)/shard_map/ppermute | solution.py:30

commit v2 on v1

v2 whole, which is shorter than its diff:
```python
import functools

import jax
import jax.numpy as jnp
from jax import lax
from jax.experimental import pallas as pl
from jax.experimental.pallas import tpu as pltpu
from jax.sharding import PartitionSpec as P

UNROLL = 16
BY_ROWS = (((1,), (0,)), ((), ()))
BY_COLS = (((1,), (1,)), ((), ()))

OUT_TURN = (4, 2, 0, 10, 13, 7, 9, 6, 12, 3, 1, 14, 8, 15, 5, 11)
IN_TURN = (4, 6, 12, 2, 0, 11, 8, 14, 5, 3, 1, 15, 13, 10, 9, 7)


def partner(turn, r, c):
    step = turn[2 * (((c >> 1) - (r >> 1)) % 8) + ((c ^ r) & 1)]
    half = (r >> 3) ^ ((step >> 1) & 1)
    return (half << 3) | ((((r >> 1) + (step >> 2)) & 3) << 1) | (step & 1)


def pairs(turn, n_row, n_col):
    return [
        (r * n_col + c, partner(turn, r, c) * n_col + r) for r in range(n_row) for c in range(n_col)
    ]


def split(value):
    high = value.astype(jnp.bfloat16)
    low = (value - high.astype(jnp.float32)).astype(jnp.bfloat16)
    return high, low


def product_body(rows_out, pos_ref, count_ref, x_ref, tile_ref, out_ref, lhs_ref):
    n_tiles, vecs, _ = x_ref.shape
    for t in range(n_tiles):
        high, low = split(x_ref[t])
        upper = jnp.concatenate([high, high], axis=1)
        lower = jnp.concatenate([low, jnp.zeros_like(low)], axis=1)
        lhs_ref[t] = jnp.concatenate([upper, lower], axis=0)
    lhs_ref[n_tiles] = jnp.zeros(lhs_ref.shape[1:], jnp.bfloat16)
    out_ref[...] = jnp.zeros_like(out_ref)
    count = count_ref[0]

    def group(g, carry):
        for u in range(UNROLL):
            slot = g * UNROLL + u
            pos = pos_ref[slot]
            row, col = pos // n_tiles, pos % n_tiles
            source, target = (col, row) if rows_out else (row, col)
            source = jnp.where(slot < count, source, n_tiles)
            rhs = jnp.concatenate(split(tile_ref[slot]), axis=1 if rows_out else 0)
            both = lax.dot_general(
                lhs_ref[source],
                rhs,
                BY_COLS if rows_out else BY_ROWS,
                preferred_element_type=jnp.float32,
            )
            out_ref[target] += both[:vecs] + both[vecs:]
        return carry

    lax.fori_loop(0, tile_ref.shape[0] // UNROLL, group, 0)


def product(rows_out, pos, count, x, tiles):
    n_tiles, vecs, width = x.shape
    smem = pl.BlockSpec(memory_space=pltpu.SMEM)
    vmem = pl.BlockSpec(memory_space=pltpu.VMEM)
    return pl.pallas_call(
        functools.partial(product_body, rows_out),
        out_shape=jax.ShapeDtypeStruct(x.shape, jnp.float32),
        in_specs=[smem, smem, vmem, vmem],
        out_specs=vmem,
        scratch_shapes=[pltpu.VMEM((n_tiles + 1, 2 * vecs, 2 * width), jnp.bfloat16)],
        compiler_params=pltpu.CompilerParams(vmem_limit_bytes=20 << 20),
        cost_estimate=pl.CostEstimate(
            flops=6 * vecs * tiles.size, bytes_accessed=4 * tiles.size, transcendentals=0
        ),
        name="row_terms" if rows_out else "col_terms",
    )(pos, count, x, tiles)


def local(vectors, tile_blocks, coords, counts):
    n_row = lax.axis_size("row")
    n_col = lax.axis_size("col")
    max_slots = tile_blocks.shape[2]
    vecs, tile = vectors.shape
    axes = ("row", "col")
    out_pairs = pairs(OUT_TURN, n_row, n_col)
    in_pairs = [(b, a) for a, b in pairs(IN_TURN, n_row, n_col)]
    tiles = tile_blocks.reshape(max_slots, tile, tile)
    pos = coords.reshape(max_slots)
    count = counts.reshape(1)

    spread = jnp.broadcast_to(vectors[None], (n_row, vecs, tile))
    x_col = lax.all_to_all(spread, "row", 0, 0, tiled=True)
    x_row = lax.ppermute(x_col, axes, in_pairs)
    row_terms = product(True, pos, count, x_col, tiles)
    moved = lax.ppermute(row_terms, axes, out_pairs)
    col_terms = product(False, pos, count, x_row, tiles)
    parts = lax.all_to_all(col_terms + moved, "row", 0, 0, tiled=True)
    return jnp.sum(parts, axis=0)


def solution(mesh):
    return jax.shard_map(
        local,
        mesh=mesh,
        in_specs=(
            P(None, ("col", "row")),
            P("row", "col", None, None, None),
            P("row", "col", None),
            P("row", "col"),
        ),
        out_specs=P(None, ("col", "row")),
        check_vma=False,
    )
```

time: 91.3 us -> 62.6 us (0.69)
  matrix products: 26.8 us -> 0 us
  Pallas kernels: 0 us -> 7.27 us
  blocking collectives: 27.6 us -> 21.1 us
  waiting for transfers between devices: 17.6 us -> 11.7 us
  local copies, waits for them, and re-layouts: 2.91 us -> 5.4 us
  starting transfers between devices: 14 us -> 15.5 us
    dot_general x4 -> x0, matrix products: 26.8 us -> none  [the longest x1 15.5 us: local(): jnp.einsum('svk,smk->svm', jnp.take(x_col, col_pos, axis=0), blocks, prec...]
    pallas_call x0 -> x2, Pallas kernels: none -> 7.27 us  [product(): pl.pallas_call(functools.partial(product_body, rows_out), out_shape=jax.S...]
    ppermute x2, waiting for transfers between devices: 11.3 us -> 4.69 us  [the longest x1 4.69 us: local(): moved = lax.ppermute(row_terms, axes, out_pairs)]
    all_to_all x1, blocking collectives: 27.6 us -> 21.1 us  [local(): parts = lax.all_to_all(col_terms + moved, 'row', 0, 0, tiled=True)]
    unnamed x0 -> x6, local copies, waits for them, and re-layouts: none -> 4.04 us
    ppermute x2, starting transfers between devices: 5.56 us -> 7.1 us  [the longest x1 7.01 us: local(): x_row = lax.ppermute(x_col, axes, in_pairs)]
    gather x2 -> x0, local copies, waits for them, and re-layouts: 1.52 us -> none  [the longest x1 0.76 us: local(): jnp.take(x_row, row_pos, axis=0)]
  transfers between devices with their start and end apart: 3 -> 3, of which waited for: 2 -> 2; matrix products, arithmetic and copies ran while one was open for 13% -> 0% of each run, Pallas kernels for 0% -> 12%
where the time goes in v2:
time: 62.6 us; the launch traced here: 62.3 us
  blocking collectives  21.1 us (34%)
  starting transfers between devices  15.5 us (25%)
  waiting for transfers between devices  11.7 us (19%)
  Pallas kernels  7.27 us (12%)
  local copies, waits for them, and re-layouts  5.4 us (9%)
  between operations  0.69 us (1%)
  other arithmetic  0.63 us (1%)
    all_to_all x1, blocking collectives, local(): parts = lax.all_to_all(col_terms + moved, 'row', 0, 0, tiled=True)  21.1 us
    all_to_all x1, starting transfers between devices, local(): x_col = lax.all_to_all(spread, 'row', 0, 0, tiled=True)  8.44 us
    pallas_call x2, Pallas kernels, product(): pl.pallas_call(functools.partial(product_body, rows_out), out_shape=jax.S...  7.27 us
    ppermute x1, starting transfers between devices, local(): x_row = lax.ppermute(x_col, axes, in_pairs)  7.01 us
    all_to_all x1, waiting for transfers between devices, local(): x_col = lax.all_to_all(spread, 'row', 0, 0, tiled=True)  6.96 us
    ppermute x1, waiting for transfers between devices, local(): moved = lax.ppermute(row_terms, axes, out_pairs)  4.69 us
    unnamed x6, local copies, waits for them, and re-layouts  4.04 us
    broadcast_in_dim x1, local copies, waits for them, and re-layouts, local(): spread = jnp.broadcast_to(vectors[None], (n_row, vecs, tile))  1.36 us
  transfers between devices with their start and end apart: 3, of which 2 were waited for; matrix products, arithmetic and copies ran while one was open for 0% of the time, Pallas kernels for 12%

profile of v2, /device:TPU:1, one launch (start us, length us, event | category | flops | bytes accessed | tf_op | source)
XLA Modules:
  0.0 62.3 jit_solution(3847685966595486295)
XLA Ops:
  0.0 1.4 %broadcast_in_dim.2 = f32[16,16,128]{2,1,0:T(8,128)} broadcast(f32[16,128]{1,0:T(8,128)} %param.4), dimensions={1,2} | broadcast | bytes 139264 | tf_op jit(solution)/shard_map/broadcast_in_dim | solution.py:97
  1.4 8.4 %all-to-all-start = ((f32[16,16,128]{2,1,0:T(8,128)}), f32[16,16,128]{2,1,0:T(8,128)S(1)}, u32[]{:S(2)}, u32[]{:S(2)}) async-start(f32[16,16,128]{2,1,0:T(8,128)} %broadcast_in_dim.2), calls=%async_computation | async-start | bytes 262144 | tf_op jit(solution)/shard_map/all_to_all | solution.py:98
  10.4 7.0 %all-to-all-done.x_ref = f32[16,16,128]{2,1,0:T(8,128)S(1)} async-done(((f32[16,16,128]{2,1,0:T(8,128)}), f32[16,16,128]{2,1,0:T(8,128)S(1)}, u32[]{:S(2)}, u32[]{:S(2)}) %all-to-all-start) | async-done | bytes 131104 | tf_op jit(solution)/shard_map/all_to_all | solution.py:98
  17.4 7.0 %collective-permute-start = (f32[16,16,128]{2,1,0:T(8,128)S(1)}, f32[16,16,128]{2,1,0:T(8,128)S(1)}, u32[]{:S(2)}, u32[]{:S(2)}) collective-permute-start(f32[16,16,128]{2,1,0:T(8,128)S(1)} %all-to-all-done.x_ref), channel_id=1, source_target_pairs={{32,0},{160,1},{96,2},{128,3},{0,4},{208,5},{64,6},{224,7},{48,8},... | collective-permute-start | bytes 393224 | tf_op jit(solution)/shard_map/ppermute | solution.py:99
  24.4 0.0 copy-start
  24.4 3.4 %copy-done = f32[1,1,128,128,128]{4,3,2,1,0:T(8,128)S(1)} copy-done((f32[1,1,128,128,128]{4,3,2,1,0:T(8,128)S(1)}, f32[1,1,128,128,128]{4,3,2,1,0:T(8,128)}, u32[]{:S(2)}) %copy-start) | copy-done | bytes 8388632
  27.8 0.0 copy-start.2
  27.8 0.7 %copy-done.2 = s32[1,1,128]{2,1,0:T(1,128)S(1)} copy-done((s32[1,1,128]{2,1,0:T(1,128)S(1)}, s32[1,1,128]{2,1,0:T(1,128)}, u32[]{:S(2)}) %copy-start.2) | copy-done | bytes 536
  28.5 0.0 copy-start.1
  28.5 4.4 %row_terms.1 = f32[16,16,128]{2,1,0:T(8,128)S(1)} custom-call(s32[128]{0:T(128)S(1)} %bitcast.7, s32[1]{0:T(128)} %bitcast.4.count_ref, f32[16,16,128]{2,1,0:T(8,128)S(1)} %all-to-all-done.x_ref, f32[128,128,128]{2,1,0:T(8,128)S(1)} %bitcast.5), custom_call_target="tpu_custom_call" | custom-call | flops 201326592 | bytes 8388608 | tf_op jit(solution)/shard_map/row_terms/pallas_call | solution.py:71
  32.9 0.1 collective-permute-start.1
  33.0 0.0 collective-permute-done.x_ref
  33.0 0.0 copy-done.1
  33.0 2.9 %col_terms.1 = f32[16,16,128]{2,1,0:T(8,128)S(1)} custom-call(s32[128]{0:T(128)S(1)} %bitcast.8, s32[1]{0:T(128)} %bitcast.3.count_ref, f32[16,16,128]{2,1,0:T(8,128)S(1)} %collective-permute-done.x_ref, f32[128,128,128]{2,1,0:T(8,128)S(1)} %bitcast.6), custom_call_target="tpu_custom_call" | custom-call | flops 201326592 | bytes 8388608 | tf_op jit(solution)/shard_map/col_terms/pallas_call | solution.py:71
  35.9 4.7 %collective-permute-done.1 = f32[16,16,128]{2,1,0:T(8,128)S(1)} collective-permute-done((f32[16,16,128]{2,1,0:T(8,128)S(1)}, f32[16,16,128]{2,1,0:T(8,128)S(1)}, u32[]{:S(2)}, u32[]{:S(2)}) %collective-permute-start.1) | collective-permute-done | bytes 131104 | tf_op jit(solution)/shard_map/ppermute | solution.py:101
  40.6 21.1 %all_to_all.10 = f32[16,16,128]{2,1,0:T(8,128)S(1)} all-to-all(f32[16,16,128]{2,1,0:T(8,128)S(1)} %add.3), channel_id=1, replica_groups=mesh['row'=16,'col'=16] {'row'}, dimensions={0} | all-to-all | bytes 262144 | tf_op jit(solution)/shard_map/all_to_all | solution.py:103
  61.7 0.6 reduce_sum.9
  (1 shorter events, 0.0 us)
Async XLA Ops:
  1.4 16.1 %all-to-all-start = ((f32[16,16,128]{2,1,0:T(8,128)}), f32[16,16,128]{2,1,0:T(8,128)S(1)}, u32[]{:S(2)}, u32[]{:S(2)}) async-start(f32[16,16,128]{2,1,0:T(8,128)} %broadcast_in_dim.2), calls=%async_computation | async-start | bytes 262144 | tf_op jit(solution)/shard_map/all_to_all | solution.py:98
  17.4 15.6 %collective-permute-start = (f32[16,16,128]{2,1,0:T(8,128)S(1)}, f32[16,16,128]{2,1,0:T(8,128)S(1)}, u32[]{:S(2)}, u32[]{:S(2)}) collective-permute-start(f32[16,16,128]{2,1,0:T(8,128)S(1)} %all-to-all-done.x_ref), channel_id=1, source_target_pairs={{32,0},{160,1},{96,2},{128,3},{0,4},{208,5},{64,6},{224,7},{48,8},... | collective-permute-start | bytes 393224 | tf_op jit(solution)/shard_map/ppermute | solution.py:99
  24.4 3.4 %copy-start = (f32[1,1,128,128,128]{4,3,2,1,0:T(8,128)S(1)}, f32[1,1,128,128,128]{4,3,2,1,0:T(8,128)}, u32[]{:S(2)}) copy-start(f32[1,1,128,128,128]{4,3,2,1,0:T(8,128)} %param.5) | copy-start | bytes 25165828
  27.8 0.7 %copy-start.2 = (s32[1,1,128]{2,1,0:T(1,128)S(1)}, s32[1,1,128]{2,1,0:T(1,128)}, u32[]{:S(2)}) copy-start(s32[1,1,128]{2,1,0:T(1,128)} %param.6) | copy-start | bytes 1540
  28.5 4.5 %copy-start.1 = (f32[1,1,128,128,128]{4,3,2,1,0:T(8,128)S(1)}, f32[1,1,128,128,128]{4,3,2,1,0:T(8,128)}, u32[]{:S(2)}) copy-start(f32[1,1,128,128,128]{4,3,2,1,0:T(8,128)} %param.5) | copy-start | bytes 25165828
  32.9 7.7 %collective-permute-start.1 = (f32[16,16,128]{2,1,0:T(8,128)S(1)}, f32[16,16,128]{2,1,0:T(8,128)S(1)}, u32[]{:S(2)}, u32[]{:S(2)}) collective-permute-start(f32[16,16,128]{2,1,0:T(8,128)S(1)} %row_terms.1), channel_id=1, source_target_pairs={{0,32},{1,128},{2,0},{3,192},{4,112},{5,176},{6,80},{7,160},{8,96}... | collective-permute-start | bytes 393224 | tf_op jit(solution)/shard_map/ppermute | solution.py:101

commit v3 on v2

v3 whole, which is shorter than its diff:
```python
import functools

import jax
import jax.numpy as jnp
from jax import lax
from jax.experimental import pallas as pl
from jax.experimental.pallas import tpu as pltpu
from jax.sharding import PartitionSpec as P


CHUNK = 16
BY_ROWS = (((1,), (0,)), ((), ()))
BY_COLS = (((1,), (1,)), ((), ()))

TURN = (4, 6, 12, 2, 0, 11, 8, 14, 5, 3, 1, 15, 13, 10, 9, 7)


def turned(r, entry):
    c = ((((r >> 1) + (entry >> 1)) & 7) << 1) | ((r ^ entry) & 1)
    step = TURN[entry]
    half = (r >> 3) ^ ((step >> 1) & 1)
    i = (half << 3) | ((((r >> 1) + (step >> 2)) & 3) << 1) | (step & 1)
    return c, i


def pairs(n_row, n_col):
    found = []
    for r in range(n_row):
        for entry in range(n_col):
            c, i = turned(r, entry)
            found.append((r * n_col + c, i * n_col + r))
    return found


def split(value):
    high = value.astype(jnp.bfloat16)
    low = (value - high.astype(jnp.float32)).astype(jnp.bfloat16)
    return high, low


def product_body(rows_out, pos_ref, count_ref, x_ref, tile_ref, out_ref, lhs_ref, place_ref, held, done):
    n_tiles, vecs, _ = x_ref.shape

    def fetch(g):
        part = pl.ds(g * CHUNK, CHUNK)
        return pltpu.make_async_copy(tile_ref.at[part], held.at[part], done.at[g])

    count = count_ref[0]
    groups = (count + CHUNK - 1) // CHUNK

    def begin(g, carry):
        fetch(g).start()
        return carry

    lax.fori_loop(0, groups, begin, 0)
    if rows_out:
        r = lax.axis_index("row")
        for entry in range(n_tiles):
            c, i = turned(r, entry)
            place_ref[i] = c
    for t in range(n_tiles):
        high, low = split(x_ref[t])
        upper = jnp.concatenate([high, high], axis=1)
        lower = jnp.concatenate([low, jnp.zeros_like(low)], axis=1)
        lhs_ref[t] = jnp.concatenate([upper, lower], axis=0)
    lhs_ref[n_tiles] = jnp.zeros(lhs_ref.shape[1:], jnp.bfloat16)
    out_ref[...] = jnp.zeros_like(out_ref)

    def group(g, carry):
        fetch(g).wait()
        for u in range(CHUNK):
            slot = g * CHUNK + u
            pos = pos_ref[slot]
            row, col = pos // n_tiles, pos % n_tiles
            source, target = (col, row) if rows_out else (row, col)
            target = place_ref[target] if rows_out else target
            source = jnp.where(slot < count, source, n_tiles)
            rhs = jnp.concatenate(split(held[slot]), axis=1 if rows_out else 0)
            both = lax.dot_general(
                lhs_ref[source],
                rhs,
                BY_COLS if rows_out else BY_ROWS,
                preferred_element_type=jnp.float32,
            )
            out_ref[target] += both[:vecs] + both[vecs:]
        return carry

    lax.fori_loop(0, groups, group, 0)


def product(rows_out, pos, count, x, tiles):
    n_tiles, vecs, width = x.shape
    smem = pl.BlockSpec(memory_space=pltpu.SMEM)
    vmem = pl.BlockSpec(memory_space=pltpu.VMEM)
    return pl.pallas_call(
        functools.partial(product_body, rows_out),
        out_shape=jax.ShapeDtypeStruct(x.shape, jnp.float32),
        in_specs=[smem, smem, vmem, pl.BlockSpec(memory_space=pltpu.HBM)],
        out_specs=vmem,
        scratch_shapes=[
            pltpu.VMEM((n_tiles + 1, 2 * vecs, 2 * width), jnp.bfloat16),
            pltpu.SMEM((n_tiles,), jnp.int32),
            pltpu.VMEM(tiles.shape, tiles.dtype),
            pltpu.SemaphoreType.DMA((tiles.shape[0] // CHUNK,)),
        ],
        compiler_params=pltpu.CompilerParams(vmem_limit_bytes=53 << 20),
        cost_estimate=pl.CostEstimate(
            flops=6 * vecs * tiles.size, bytes_accessed=4 * tiles.size, transcendentals=0
        ),
        name="row_terms" if rows_out else "col_terms",
    )(pos, count, x, tiles)


def local(vectors, tile_blocks, coords, counts):
    n_row = lax.axis_size("row")
    n_col = lax.axis_size("col")
    max_slots = tile_blocks.shape[2]
    vecs, tile = vectors.shape
    axes = ("row", "col")
    turn = pairs(n_row, n_col)
    tiles = tile_blocks.reshape(max_slots, tile, tile)
    pos = coords.reshape(max_slots)
    count = counts.reshape(1)

    spread = jnp.broadcast_to(vectors[None], (n_row, vecs, tile))
    x_col = lax.all_to_all(spread, "row", 0, 0, tiled=True)
    x_row = lax.ppermute(x_col, axes, [(b, a) for a, b in turn])
    row_terms = product(True, pos, count, x_col, tiles)
    row_parts = lax.all_to_all(row_terms, "col", 0, 0, tiled=True)
    col_terms = product(False, pos, count, x_row, tiles)
    col_parts = lax.all_to_all(col_terms, "row", 0, 0, tiled=True)
    row_sum = lax.ppermute(jnp.sum(row_parts, axis=0), axes, turn)
    return jnp.sum(col_parts, axis=0) + row_sum


def solution(mesh):
    return jax.shard_map(
        local,
        mesh=mesh,
        in_specs=(
            P(None, ("col", "row")),
            P("row", "col", None, None, None),
            P("row", "col", None),
            P("row", "col"),
        ),
        out_specs=P(None, ("col", "row")),
        check_vma=False,
    )
```

time: 62.6 us -> 66.1 us (1.056)
  the two profiles are of different devices: /device:TPU:1 before, /device:TPU:31 now
where the time goes in v3:
time: 66.1 us; the launch traced here: 65.7 us
  starting transfers between devices  34.8 us (53%)
  waiting for transfers between devices  16.2 us (25%)
  Pallas kernels  11.3 us (17%)
  local copies, waits for them, and re-layouts  2.03 us (3%)
  between operations  0.69 us (1%)
    pallas_call x2, Pallas kernels, product(): pl.pallas_call(functools.partial(product_body, rows_out), out_shape=jax.S...  11.3 us
    all_to_all x1, starting transfers between devices, local(): col_parts = lax.all_to_all(col_terms, 'row', 0, 0, tiled=True)  11 us
    all_to_all x1, starting transfers between devices, local(): row_parts = lax.all_to_all(row_terms, 'col', 0, 0, tiled=True)  8.94 us
    all_to_all x1, starting transfers between devices, local(): x_col = lax.all_to_all(spread, 'row', 0, 0, tiled=True)  7.4 us
    ppermute x1, starting transfers between devices, local(): x_row = lax.ppermute(x_col, axes, [(b, a) for a, b in turn])  6.5 us
    ppermute x1, waiting for transfers between devices, local(): row_sum = lax.ppermute(jnp.sum(row_parts, axis=0), axes, turn)  6.08 us
    ppermute x1, waiting for transfers between devices, local(): x_row = lax.ppermute(x_col, axes, [(b, a) for a, b in turn])  4.32 us
    all_to_all x1, waiting for transfers between devices, local(): x_col = lax.all_to_all(spread, 'row', 0, 0, tiled=True)  3.08 us
  transfers between devices with their start and end apart: 5, of which 4 were waited for; matrix products, arithmetic and copies ran while one was open for 0% of the time, Pallas kernels for 8%

profile of v3, /device:TPU:31, one launch (start us, length us, event | category | flops | bytes accessed | tf_op | source)
XLA Modules:
  0.0 65.7 jit_solution(1679101409188524651)
XLA Ops:
  0.0 0.0 copy-start.1
  0.0 1.4 %broadcast_in_dim.2 = f32[16,16,128]{2,1,0:T(8,128)} broadcast(f32[16,128]{1,0:T(8,128)} %param.4), dimensions={1,2} | broadcast | bytes 139264 | tf_op jit(solution)/shard_map/broadcast_in_dim | solution.py:125
  1.4 7.4 %all-to-all-start = ((f32[16,16,128]{2,1,0:T(8,128)}), f32[16,16,128]{2,1,0:T(8,128)S(1)}, u32[]{:S(2)}, u32[]{:S(2)}) async-start(f32[16,16,128]{2,1,0:T(8,128)} %broadcast_in_dim.2), calls=%async_computation | async-start | bytes 262144 | tf_op jit(solution)/shard_map/all_to_all | solution.py:126
  9.4 3.1 %all-to-all-done.x_ref = f32[16,16,128]{2,1,0:T(8,128)S(1)} async-done(((f32[16,16,128]{2,1,0:T(8,128)}), f32[16,16,128]{2,1,0:T(8,128)S(1)}, u32[]{:S(2)}, u32[]{:S(2)}) %all-to-all-start) | async-done | bytes 131104 | tf_op jit(solution)/shard_map/all_to_all | solution.py:126
  12.5 0.0 copy-start
  12.5 0.7 copy-done
  13.2 6.3 %row_terms.1 = f32[16,16,128]{2,1,0:T(8,128)} custom-call(s32[128]{0:T(128)S(1)} %bitcast.5, s32[1]{0:T(128)} %bitcast.4.count_ref, f32[16,16,128]{2,1,0:T(8,128)S(1)} %all-to-all-done.x_ref, f32[128,128,128]{2,1,0:T(8,128)} %bitcast.7), custom_call_target="tpu_custom_call" | custom-call | flops 201326592 | bytes 8388608 | tf_op jit(solution)/shard_map/row_terms/pallas_call | solution.py:95
  19.5 8.9 %all-to-all-start.2 = ((f32[16,16,128]{2,1,0:T(8,128)}), f32[16,16,128]{2,1,0:T(8,128)S(1)}, u32[]{:S(2)}, u32[]{:S(2)}) async-start(f32[16,16,128]{2,1,0:T(8,128)} %row_terms.1), calls=%async_computation.2 | async-start | bytes 262144 | tf_op jit(solution)/shard_map/all_to_all | solution.py:129
  28.4 6.5 %collective-permute-start = (f32[16,16,128]{2,1,0:T(8,128)S(1)}, f32[16,16,128]{2,1,0:T(8,128)S(1)}, u32[]{:S(2)}, u32[]{:S(2)}) collective-permute-start(f32[16,16,128]{2,1,0:T(8,128)S(1)} %all-to-all-done.x_ref), channel_id=1, source_target_pairs={{32,0},{160,1},{96,2},{128,3},{0,4},{208,5},{64,6},{224,7},{48,8},... | collective-permute-start | bytes 393224 | tf_op jit(solution)/shard_map/ppermute | solution.py:127
  34.9 4.3 %collective-permute-done.x_ref = f32[16,16,128]{2,1,0:T(8,128)S(1)} collective-permute-done((f32[16,16,128]{2,1,0:T(8,128)S(1)}, f32[16,16,128]{2,1,0:T(8,128)S(1)}, u32[]{:S(2)}, u32[]{:S(2)}) %collective-permute-start) | collective-permute-done | bytes 131104 | tf_op jit(solution)/shard_map/ppermute | solution.py:127
  39.2 0.0 copy-done.1
  39.2 5.0 %col_terms.1 = f32[16,16,128]{2,1,0:T(8,128)} custom-call(s32[128]{0:T(128)S(1)} %bitcast.6, s32[1]{0:T(128)} %bitcast.3.count_ref, f32[16,16,128]{2,1,0:T(8,128)S(1)} %collective-permute-done.x_ref, f32[128,128,128]{2,1,0:T(8,128)} %bitcast.8), custom_call_target="tpu_custom_call" | custom-call | flops 201326592 | bytes 8388608 | tf_op jit(solution)/shard_map/col_terms/pallas_call | solution.py:95
  44.2 0.0 all-to-all-done.2
  44.2 11.0 %all-to-all-start.1 = ((f32[16,16,128]{2,1,0:T(8,128)}), f32[16,16,128]{2,1,0:T(8,128)S(1)}, u32[]{:S(2)}, u32[]{:S(2)}) async-start(f32[16,16,128]{2,1,0:T(8,128)} %col_terms.1), calls=%async_computation.1 | async-start | bytes 262144 | tf_op jit(solution)/shard_map/all_to_all | solution.py:131
  55.3 0.9 %collective-permute-start.1 = (f32[16,128]{1,0:T(8,128)S(1)}, f32[16,128]{1,0:T(8,128)S(1)}, u32[]{:S(2)}, u32[]{:S(2)}) collective-permute-start(f32[16,128]{1,0:T(8,128)S(1)} %reduce_sum.19), channel_id=1, source_target_pairs={{0,32},{1,160},{2,96},{3,128},{4,0},{5,208},{6,64},{7,224},{8,48},... | collective-permute-start | bytes 24584 | tf_op jit(solution)/shard_map/ppermute | solution.py:132
  56.2 2.8 %all-to-all-done.1 = f32[16,16,128]{2,1,0:T(8,128)S(1)} async-done(((f32[16,16,128]{2,1,0:T(8,128)}), f32[16,16,128]{2,1,0:T(8,128)S(1)}, u32[]{:S(2)}, u32[]{:S(2)}) %all-to-all-start.1) | async-done | bytes 131104 | tf_op jit(solution)/shard_map/all_to_all | solution.py:131
  59.0 6.1 %collective-permute-done.1 = f32[16,128]{1,0:T(8,128)S(1)} collective-permute-done((f32[16,128]{1,0:T(8,128)S(1)}, f32[16,128]{1,0:T(8,128)S(1)}, u32[]{:S(2)}, u32[]{:S(2)}) %collective-permute-start.1) | collective-permute-done | bytes 8224 | tf_op jit(solution)/shard_map/ppermute | solution.py:132
  65.1 0.6 add.3
  (2 shorter events, 0.0 us)
Async XLA Ops:
  0.0 39.2 %copy-start.1 = (s32[1,1,128]{2,1,0:T(1,128)S(1)}, s32[1,1,128]{2,1,0:T(1,128)}, u32[]{:S(2)}) copy-start(s32[1,1,128]{2,1,0:T(1,128)} %param.6) | copy-start | bytes 1540
  1.4 11.1 %all-to-all-start = ((f32[16,16,128]{2,1,0:T(8,128)}), f32[16,16,128]{2,1,0:T(8,128)S(1)}, u32[]{:S(2)}, u32[]{:S(2)}) async-start(f32[16,16,128]{2,1,0:T(8,128)} %broadcast_in_dim.2), calls=%async_computation | async-start | bytes 262144 | tf_op jit(solution)/shard_map/all_to_all | solution.py:126
  12.5 0.7 copy-start
  19.5 24.7 %all-to-all-start.2 = ((f32[16,16,128]{2,1,0:T(8,128)}), f32[16,16,128]{2,1,0:T(8,128)S(1)}, u32[]{:S(2)}, u32[]{:S(2)}) async-start(f32[16,16,128]{2,1,0:T(8,128)} %row_terms.1), calls=%async_computation.2 | async-start | bytes 262144 | tf_op jit(solution)/shard_map/all_to_all | solution.py:129
  28.4 10.8 %collective-permute-start = (f32[16,16,128]{2,1,0:T(8,128)S(1)}, f32[16,16,128]{2,1,0:T(8,128)S(1)}, u32[]{:S(2)}, u32[]{:S(2)}) collective-permute-start(f32[16,16,128]{2,1,0:T(8,128)S(1)} %all-to-all-done.x_ref), channel_id=1, source_target_pairs={{32,0},{160,1},{96,2},{128,3},{0,4},{208,5},{64,6},{224,7},{48,8},... | collective-permute-start | bytes 393224 | tf_op jit(solution)/shard_map/ppermute | solution.py:127
  44.2 14.7 %all-to-all-start.1 = ((f32[16,16,128]{2,1,0:T(8,128)}), f32[16,16,128]{2,1,0:T(8,128)S(1)}, u32[]{:S(2)}, u32[]{:S(2)}) async-start(f32[16,16,128]{2,1,0:T(8,128)} %col_terms.1), calls=%async_computation.1 | async-start | bytes 262144 | tf_op jit(solution)/shard_map/all_to_all | solution.py:131
  55.3 9.8 %collective-permute-start.1 = (f32[16,128]{1,0:T(8,128)S(1)}, f32[16,128]{1,0:T(8,128)S(1)}, u32[]{:S(2)}, u32[]{:S(2)}) collective-permute-start(f32[16,128]{1,0:T(8,128)S(1)} %reduce_sum.19), channel_id=1, source_target_pairs={{0,32},{1,160},{2,96},{3,128},{4,0},{5,208},{6,64},{7,224},{8,48},... | collective-permute-start | bytes 24584 | tf_op jit(solution)/shard_map/ppermute | solution.py:132

commit v4 on v3

--- a/solution.py
+++ b/solution.py
@@ -38,21 +38,25 @@
     return high, low
 
 
-def product_body(rows_out, pos_ref, count_ref, x_ref, tile_ref, out_ref, lhs_ref, place_ref, held, done):
+def product_body(
+    rows_out, plan, count_ref, x_ref, tiles, out_ref, lhs_ref, place_ref, held, pos_ref, done
+):
     n_tiles, vecs, _ = x_ref.shape
+    bits = n_tiles.bit_length() - 1
+    count = count_ref[0, 0]
+    groups = lax.div(count + (CHUNK - 1), CHUNK)
+    pos_copy = pltpu.make_async_copy(plan, pos_ref, done.at[held.shape[0] // CHUNK])
+    pos_copy.start()
 
     def fetch(g):
         part = pl.ds(g * CHUNK, CHUNK)
-        return pltpu.make_async_copy(tile_ref.at[part], held.at[part], done.at[g])
+        return pltpu.make_async_copy(tiles.at[part], held.at[part], done.at[g])
 
-    count = count_ref[0]
-    groups = (count + CHUNK - 1) // CHUNK
-
-    def begin(g, carry):
+    def ask(g, carry):
         fetch(g).start()
         return carry
 
-    lax.fori_loop(0, groups, begin, 0)
+    lax.fori_loop(0, groups, ask, 0)
     if rows_out:
         r = lax.axis_index("row")
         for entry in range(n_tiles):
@@ -65,15 +69,15 @@
         lhs_ref[t] = jnp.concatenate([upper, lower], axis=0)
     lhs_ref[n_tiles] = jnp.zeros(lhs_ref.shape[1:], jnp.bfloat16)
     out_ref[...] = jnp.zeros_like(out_ref)
+    pos_copy.wait()
 
     def group(g, carry):
         fetch(g).wait()
         for u in range(CHUNK):
             slot = g * CHUNK + u
-            pos = pos_ref[slot]
-            row, col = pos // n_tiles, pos % n_tiles
-            source, target = (col, row) if rows_out else (row, col)
-            target = place_ref[target] if rows_out else target
+            pos = pos_ref[0, 0, slot]
+            row, col = lax.shift_right_logical(pos, bits), lax.bitwise_and(pos, n_tiles - 1)
+            source, target = (col, place_ref[row]) if rows_out else (row, col)
             source = jnp.where(slot < count, source, n_tiles)
             rhs = jnp.concatenate(split(held[slot]), axis=1 if rows_out else 0)
             both = lax.dot_general(
@@ -88,46 +92,66 @@
     lax.fori_loop(0, groups, group, 0)
 
 
-def product(rows_out, pos, count, x, tiles):
+def product(rows_out, plan, count, x, tiles):
     n_tiles, vecs, width = x.shape
+    anywhere = pl.BlockSpec(memory_space=pl.ANY)
     smem = pl.BlockSpec(memory_space=pltpu.SMEM)
     vmem = pl.BlockSpec(memory_space=pltpu.VMEM)
     return pl.pallas_call(
         functools.partial(product_body, rows_out),
         out_shape=jax.ShapeDtypeStruct(x.shape, jnp.float32),
-        in_specs=[smem, smem, vmem, pl.BlockSpec(memory_space=pltpu.HBM)],
+        in_specs=[anywhere, smem, vmem, anywhere],
         out_specs=vmem,
         scratch_shapes=[
             pltpu.VMEM((n_tiles + 1, 2 * vecs, 2 * width), jnp.bfloat16),
             pltpu.SMEM((n_tiles,), jnp.int32),
             pltpu.VMEM(tiles.shape, tiles.dtype),
-            pltpu.SemaphoreType.DMA((tiles.shape[0] // CHUNK,)),
+            pltpu.SMEM(plan.shape, plan.dtype),
+            pltpu.SemaphoreType.DMA((tiles.shape[0] // CHUNK + 1,)),
         ],
         compiler_params=pltpu.CompilerParams(vmem_limit_bytes=53 << 20),
         cost_estimate=pl.CostEstimate(
             flops=6 * vecs * tiles.size, bytes_accessed=4 * tiles.size, transcendentals=0
         ),
         name="row_terms" if rows_out else "col_terms",
-    )(pos, count, x, tiles)
+    )(plan, count, x, tiles)
+
+
+def begin_body(count_ref, coords_ref, x_ref, out_ref, plan_ref):
+    plan_ref[...] = coords_ref[...]
+    out_ref[...] = jnp.broadcast_to(x_ref[...][None], out_ref.shape)
+
+
+def begin(count, coords, x, n_copies):
+    vmem = pl.BlockSpec(memory_space=pltpu.VMEM)
+    return pl.pallas_call(
+        begin_body,
+        out_shape=(
+            jax.ShapeDtypeStruct((n_copies, *x.shape), x.dtype),
+            jax.ShapeDtypeStruct(coords.shape, coords.dtype),
+        ),
+        in_specs=[pl.BlockSpec(memory_space=pltpu.SMEM), vmem, vmem],
+        out_specs=(vmem, vmem),
+        compiler_params=pltpu.CompilerParams(vmem_limit_bytes=4 << 20),
+        name="begin",
+    )(count, coords, x)
 
 
 def local(vectors, tile_blocks, coords, counts):
     n_row = lax.axis_size("row")
     n_col = lax.axis_size("col")
     max_slots = tile_blocks.shape[2]
-    vecs, tile = vectors.shape
+    _, tile = vectors.shape
     axes = ("row", "col")
     turn = pairs(n_row, n_col)
     tiles = tile_blocks.reshape(max_slots, tile, tile)
-    pos = coords.reshape(max_slots)
-    count = counts.reshape(1)
 
-    spread = jnp.broadcast_to(vectors[None], (n_row, vecs, tile))
+    spread, plan = begin(counts, coords, vectors, n_row)
     x_col = lax.all_to_all(spread, "row", 0, 0, tiled=True)
     x_row = lax.ppermute(x_col, axes, [(b, a) for a, b in turn])
-    row_terms = product(True, pos, count, x_col, tiles)
+    row_terms = product(True, plan, counts, x_col, tiles)
     row_parts = lax.all_to_all(row_terms, "col", 0, 0, tiled=True)
-    col_terms = product(False, pos, count, x_row, tiles)
+    col_terms = product(False, plan, counts, x_row, tiles)
     col_parts = lax.all_to_all(col_terms, "row", 0, 0, tiled=True)
     row_sum = lax.ppermute(jnp.sum(row_parts, axis=0), axes, turn)
     return jnp.sum(col_parts, axis=0) + row_sum

time: 66.1 us -> 64.7 us (0.979)
  blocking collectives: 0 us -> 10.9 us
  starting transfers between devices: 34.8 us -> 27.4 us
  waiting for transfers between devices: 16.2 us -> 13.2 us
  Pallas kernels: 11.3 us -> 10.2 us
  local copies, waits for them, and re-layouts: 2.03 us -> 1.34 us
    all_to_all x0 -> x1, blocking collectives: none -> 10.9 us  [local(): x_col = lax.all_to_all(spread, 'row', 0, 0, tiled=True)]
    all_to_all x1 -> x0, starting transfers between devices: 7.4 us -> none  [local(): x_col = lax.all_to_all(spread, 'row', 0, 0, tiled=True)]
    all_to_all x1 -> x0, waiting for transfers between devices: 3.08 us -> none  [local(): x_col = lax.all_to_all(spread, 'row', 0, 0, tiled=True)]
    broadcast_in_dim x1 -> x0, local copies, waits for them, and re-layouts: 1.37 us -> none  [local(): spread = jnp.broadcast_to(vectors[None], (n_row, vecs, tile))]
    pallas_call x2, Pallas kernels: 11.3 us -> 10.2 us  [product(): pl.pallas_call(functools.partial(product_body, rows_out), out_shape=jax.S...]
    unnamed x4, local copies, waits for them, and re-layouts: 0.66 us -> 1.34 us
  transfers between devices with their start and end apart: 5 -> 4, of which waited for: 4 -> 3; matrix products, arithmetic and copies ran while one was open for 0% -> 0% of each run, Pallas kernels for 8% -> 7%
where the time goes in v4:
time: 64.7 us; the launch traced here: 64.3 us
  starting transfers between devices  27.4 us (42%)
  waiting for transfers between devices  13.2 us (20%)
  blocking collectives  10.9 us (17%)
  Pallas kernels  10.2 us (16%)
  local copies, waits for them, and re-layouts  1.34 us (2%)
  between operations  0.7 us (1%)
    all_to_all x1, starting transfers between devices, local(): col_parts = lax.all_to_all(col_terms, 'row', 0, 0, tiled=True)  11 us
    all_to_all x1, blocking collectives, local(): x_col = lax.all_to_all(spread, 'row', 0, 0, tiled=True)  10.9 us
    pallas_call x2, Pallas kernels, product(): pl.pallas_call(functools.partial(product_body, rows_out), out_shape=jax.S...  10.2 us
    all_to_all x1, starting transfers between devices, local(): row_parts = lax.all_to_all(row_terms, 'col', 0, 0, tiled=True)  8.94 us
    ppermute x1, starting transfers between devices, local(): x_row = lax.ppermute(x_col, axes, [(b, a) for a, b in turn])  6.49 us
    ppermute x1, waiting for transfers between devices, local(): row_sum = lax.ppermute(jnp.sum(row_parts, axis=0), axes, turn)  6.08 us
    ppermute x1, waiting for transfers between devices, local(): x_row = lax.ppermute(x_col, axes, [(b, a) for a, b in turn])  4.32 us
    all_to_all x1, waiting for transfers between devices, local(): col_parts = lax.all_to_all(col_terms, 'row', 0, 0, tiled=True)  2.76 us
  transfers between devices with their start and end apart: 4, of which 3 were waited for; matrix products, arithmetic and copies ran while one was open for 0% of the time, Pallas kernels for 7%

profile of v4, /device:TPU:31, one launch (start us, length us, event | category | flops | bytes accessed | tf_op | source)
XLA Modules:
  0.0 64.3 jit_solution(2600978421028816230)
XLA Ops:
  0.7 0.0 copy-start
  0.7 0.7 %copy-done = f32[16,128]{1,0:T(8,128)S(1)} copy-done((f32[16,128]{1,0:T(8,128)S(1)}, f32[16,128]{1,0:T(8,128)}, u32[]{:S(2)}) %copy-start) | copy-done | bytes 8216
  1.4 0.0 copy-start.1
  1.4 0.7 %copy-done.1 = s32[1,1,128]{2,1,0:T(1,128)S(1)} copy-done((s32[1,1,128]{2,1,0:T(1,128)S(1)}, s32[1,1,128]{2,1,0:T(1,128)}, u32[]{:S(2)}) %copy-start.1) | copy-done | bytes 536
  2.0 10.9 %all_to_all.15.x_ref = f32[16,16,128]{2,1,0:T(8,128)S(1)} all-to-all(f32[16,16,128]{2,1,0:T(8,128)S(1)} %get-tuple-element.8), channel_id=1, replica_groups=mesh['row'=16,'col'=16] {'row'}, dimensions={0} | all-to-all | bytes 262144 | tf_op jit(solution)/shard_map/all_to_all | solution.py:150
  12.9 5.8 %row_terms.1 = f32[16,16,128]{2,1,0:T(8,128)} custom-call(s32[1,1,128]{2,1,0:T(1,128)S(1)} %get-tuple-element.7.plan, s32[1,1]{1,0:T(1,128)S(6)} %copy.5.count_ref, f32[16,16,128]{2,1,0:T(8,128)S(1)} %all_to_all.15.x_ref, f32[128,128,128]{2,1,0:T(8,128)} %bitcast.1), custom_call_target="tpu_custom_call" | custom-call | flops 201326592 | bytes 8388608 | tf_op jit(solution)/shard_map/row_terms/pallas_call | solution.py:100
  18.7 8.9 %all-to-all-start.2 = ((f32[16,16,128]{2,1,0:T(8,128)}), f32[16,16,128]{2,1,0:T(8,128)S(1)}, u32[]{:S(2)}, u32[]{:S(2)}) async-start(f32[16,16,128]{2,1,0:T(8,128)} %row_terms.1), calls=%async_computation.2 | async-start | bytes 262144 | tf_op jit(solution)/shard_map/all_to_all | solution.py:153
  27.7 6.5 %collective-permute-start = (f32[16,16,128]{2,1,0:T(8,128)S(1)}, f32[16,16,128]{2,1,0:T(8,128)S(1)}, u32[]{:S(2)}, u32[]{:S(2)}) collective-permute-start(f32[16,16,128]{2,1,0:T(8,128)S(1)} %all_to_all.15.x_ref), channel_id=1, source_target_pairs={{32,0},{160,1},{96,2},{128,3},{0,4},{208,5},{64,6},{224,7},{48,8},... | collective-permute-start | bytes 393224 | tf_op jit(solution)/shard_map/ppermute | solution.py:151
  34.1 4.3 %collective-permute-done.x_ref = f32[16,16,128]{2,1,0:T(8,128)S(1)} collective-permute-done((f32[16,16,128]{2,1,0:T(8,128)S(1)}, f32[16,16,128]{2,1,0:T(8,128)S(1)}, u32[]{:S(2)}, u32[]{:S(2)}) %collective-permute-start) | collective-permute-done | bytes 131104 | tf_op jit(solution)/shard_map/ppermute | solution.py:151
  38.5 4.4 %col_terms.1 = f32[16,16,128]{2,1,0:T(8,128)} custom-call(s32[1,1,128]{2,1,0:T(1,128)S(1)} %get-tuple-element.7.plan, s32[1,1]{1,0:T(1,128)S(6)} %copy.5.count_ref, f32[16,16,128]{2,1,0:T(8,128)S(1)} %collective-permute-done.x_ref, f32[128,128,128]{2,1,0:T(8,128)} %bitcast.2), custom_call_target="tpu_custom_call" | custom-call | flops 201326592 | bytes 8388608 | tf_op jit(solution)/shard_map/col_terms/pallas_call | solution.py:100
  42.9 0.0 all-to-all-done.2
  42.9 11.0 %all-to-all-start.1 = ((f32[16,16,128]{2,1,0:T(8,128)}), f32[16,16,128]{2,1,0:T(8,128)S(1)}, u32[]{:S(2)}, u32[]{:S(2)}) async-start(f32[16,16,128]{2,1,0:T(8,128)} %col_terms.1), calls=%async_computation.1 | async-start | bytes 262144 | tf_op jit(solution)/shard_map/all_to_all | solution.py:155
  53.9 1.0 %collective-permute-start.1 = (f32[16,128]{1,0:T(8,128)S(1)}, f32[16,128]{1,0:T(8,128)S(1)}, u32[]{:S(2)}, u32[]{:S(2)}) collective-permute-start(f32[16,128]{1,0:T(8,128)S(1)} %reduce_sum.19), channel_id=1, source_target_pairs={{0,32},{1,160},{2,96},{3,128},{4,0},{5,208},{6,64},{7,224},{8,48},... | collective-permute-start | bytes 24584 | tf_op jit(solution)/shard_map/ppermute | solution.py:156
  54.9 2.8 %all-to-all-done.1 = f32[16,16,128]{2,1,0:T(8,128)S(1)} async-done(((f32[16,16,128]{2,1,0:T(8,128)}), f32[16,16,128]{2,1,0:T(8,128)S(1)}, u32[]{:S(2)}, u32[]{:S(2)}) %all-to-all-start.1) | async-done | bytes 131104 | tf_op jit(solution)/shard_map/all_to_all | solution.py:155
  57.7 6.1 %collective-permute-done.1 = f32[16,128]{1,0:T(8,128)S(1)} collective-permute-done((f32[16,128]{1,0:T(8,128)S(1)}, f32[16,128]{1,0:T(8,128)S(1)}, u32[]{:S(2)}, u32[]{:S(2)}) %collective-permute-start.1) | collective-permute-done | bytes 8224 | tf_op jit(solution)/shard_map/ppermute | solution.py:156
  63.7 0.6 add.3
  (3 shorter events, 0.0 us)
Async XLA Ops:
  0.7 0.7 %copy-start = (f32[16,128]{1,0:T(8,128)S(1)}, f32[16,128]{1,0:T(8,128)}, u32[]{:S(2)}) copy-start(f32[16,128]{1,0:T(8,128)} %x_ref.1) | copy-start | bytes 24580
  1.4 0.7 %copy-start.1 = (s32[1,1,128]{2,1,0:T(1,128)S(1)}, s32[1,1,128]{2,1,0:T(1,128)}, u32[]{:S(2)}) copy-start(s32[1,1,128]{2,1,0:T(1,128)} %coords_ref.1) | copy-start | bytes 1540
  18.7 24.2 %all-to-all-start.2 = ((f32[16,16,128]{2,1,0:T(8,128)}), f32[16,16,128]{2,1,0:T(8,128)S(1)}, u32[]{:S(2)}, u32[]{:S(2)}) async-start(f32[16,16,128]{2,1,0:T(8,128)} %row_terms.1), calls=%async_computation.2 | async-start | bytes 262144 | tf_op jit(solution)/shard_map/all_to_all | solution.py:153
  27.7 10.8 %collective-permute-start = (f32[16,16,128]{2,1,0:T(8,128)S(1)}, f32[16,16,128]{2,1,0:T(8,128)S(1)}, u32[]{:S(2)}, u32[]{:S(2)}) collective-permute-start(f32[16,16,128]{2,1,0:T(8,128)S(1)} %all_to_all.15.x_ref), channel_id=1, source_target_pairs={{32,0},{160,1},{96,2},{128,3},{0,4},{208,5},{64,6},{224,7},{48,8},... | collective-permute-start | bytes 393224 | tf_op jit(solution)/shard_map/ppermute | solution.py:151
  42.9 14.7 %all-to-all-start.1 = ((f32[16,16,128]{2,1,0:T(8,128)}), f32[16,16,128]{2,1,0:T(8,128)S(1)}, u32[]{:S(2)}, u32[]{:S(2)}) async-start(f32[16,16,128]{2,1,0:T(8,128)} %col_terms.1), calls=%async_computation.1 | async-start | bytes 262144 | tf_op jit(solution)/shard_map/all_to_all | solution.py:155
  53.9 9.8 %collective-permute-start.1 = (f32[16,128]{1,0:T(8,128)S(1)}, f32[16,128]{1,0:T(8,128)S(1)}, u32[]{:S(2)}, u32[]{:S(2)}) collective-permute-start(f32[16,128]{1,0:T(8,128)S(1)} %reduce_sum.19), channel_id=1, source_target_pairs={{0,32},{1,160},{2,96},{3,128},{4,0},{5,208},{6,64},{7,224},{8,48},... | collective-permute-start | bytes 24584 | tf_op jit(solution)/shard_map/ppermute | solution.py:156

commit v5 on v4

--- a/solution.py
+++ b/solution.py
@@ -76,9 +76,10 @@
         for u in range(CHUNK):
             slot = g * CHUNK + u
             pos = pos_ref[0, 0, slot]
-            row, col = lax.shift_right_logical(pos, bits), lax.bitwise_and(pos, n_tiles - 1)
+            row = lax.bitwise_and(lax.shift_right_logical(pos, bits), n_tiles - 1)
+            col = lax.bitwise_and(pos, n_tiles - 1)
             source, target = (col, place_ref[row]) if rows_out else (row, col)
-            source = jnp.where(slot < count, source, n_tiles)
+            source = jnp.where(pos < 0, n_tiles, source)
             rhs = jnp.concatenate(split(held[slot]), axis=1 if rows_out else 0)
             both = lax.dot_general(
                 lhs_ref[source],
@@ -117,36 +118,18 @@
     )(plan, count, x, tiles)
 
 
-def begin_body(count_ref, coords_ref, x_ref, out_ref, plan_ref):
-    plan_ref[...] = coords_ref[...]
-    out_ref[...] = jnp.broadcast_to(x_ref[...][None], out_ref.shape)
-
-
-def begin(count, coords, x, n_copies):
-    vmem = pl.BlockSpec(memory_space=pltpu.VMEM)
-    return pl.pallas_call(
-        begin_body,
-        out_shape=(
-            jax.ShapeDtypeStruct((n_copies, *x.shape), x.dtype),
-            jax.ShapeDtypeStruct(coords.shape, coords.dtype),
-        ),
-        in_specs=[pl.BlockSpec(memory_space=pltpu.SMEM), vmem, vmem],
-        out_specs=(vmem, vmem),
-        compiler_params=pltpu.CompilerParams(vmem_limit_bytes=4 << 20),
-        name="begin",
-    )(count, coords, x)
-
-
 def local(vectors, tile_blocks, coords, counts):
     n_row = lax.axis_size("row")
     n_col = lax.axis_size("col")
     max_slots = tile_blocks.shape[2]
-    _, tile = vectors.shape
+    vecs, tile = vectors.shape
     axes = ("row", "col")
     turn = pairs(n_row, n_col)
     tiles = tile_blocks.reshape(max_slots, tile, tile)
 
-    spread, plan = begin(counts, coords, vectors, n_row)
+    spread = jnp.broadcast_to(vectors[None], (n_row, vecs, tile))
+    slots = jnp.arange(max_slots, dtype=jnp.int32)
+    plan = jnp.where(slots < counts[:, :, None], coords, -1)
     x_col = lax.all_to_all(spread, "row", 0, 0, tiled=True)
     x_row = lax.ppermute(x_col, axes, [(b, a) for a, b in turn])
     row_terms = product(True, plan, counts, x_col, tiles)

time: 64.7 us -> 64.3 us (level)
  blocking collectives: 10.9 us -> 0 us
  starting transfers between devices: 27.4 us -> 34.8 us
  waiting for transfers between devices: 13.2 us -> 15.6 us
  other arithmetic: 0.64 us -> 1.3 us
    all_to_all x1 -> x0, blocking collectives: 10.9 us -> none  [local(): x_col = lax.all_to_all(spread, 'row', 0, 0, tiled=True)]
    all_to_all x0 -> x1, starting transfers between devices: none -> 7.4 us  [local(): x_col = lax.all_to_all(spread, 'row', 0, 0, tiled=True)]
    all_to_all x0 -> x1, waiting for transfers between devices: none -> 2.42 us  [local(): x_col = lax.all_to_all(spread, 'row', 0, 0, tiled=True)]
    broadcast_in_dim x0 -> x1, local copies, waits for them, and re-layouts: none -> 1.35 us  [local(): spread = jnp.broadcast_to(vectors[None], (n_row, vecs, tile))]
    unnamed x4 -> x0, local copies, waits for them, and re-layouts: 1.34 us -> none
    select_n x0 -> x1, other arithmetic: none -> 0.66 us  [local(): plan = jnp.where(slots < counts[:, :, None], coords, -1)]
  transfers between devices with their start and end apart: 4 -> 5, of which waited for: 3 -> 4; matrix products, arithmetic and copies ran while one was open for 0% -> 1% of each run, Pallas kernels for 7% -> 7%
where the time goes in v5:
time: 64.3 us; the launch traced here: 63.9 us
  starting transfers between devices  34.8 us (54%)
  waiting for transfers between devices  15.6 us (24%)
  Pallas kernels  10.2 us (16%)
  local copies, waits for them, and re-layouts  1.35 us (2%)
  other arithmetic  1.3 us (2%)
  between operations  0.69 us (1%)
    all_to_all x1, starting transfers between devices, local(): col_parts = lax.all_to_all(col_terms, 'row', 0, 0, tiled=True)  11 us
    pallas_call x2, Pallas kernels, product(): pl.pallas_call(functools.partial(product_body, rows_out), out_shape=jax.S...  10.2 us
    all_to_all x1, starting transfers between devices, local(): row_parts = lax.all_to_all(row_terms, 'col', 0, 0, tiled=True)  8.94 us
    all_to_all x1, starting transfers between devices, local(): x_col = lax.all_to_all(spread, 'row', 0, 0, tiled=True)  7.4 us
    ppermute x1, starting transfers between devices, local(): x_row = lax.ppermute(x_col, axes, [(b, a) for a, b in turn])  6.49 us
    ppermute x1, waiting for transfers between devices, local(): row_sum = lax.ppermute(jnp.sum(row_parts, axis=0), axes, turn)  6.08 us
    ppermute x1, waiting for transfers between devices, local(): x_row = lax.ppermute(x_col, axes, [(b, a) for a, b in turn])  4.32 us
    all_to_all x1, waiting for transfers between devices, local(): col_parts = lax.all_to_all(col_terms, 'row', 0, 0, tiled=True)  2.77 us
  transfers between devices with their start and end apart: 5, of which 4 were waited for; matrix products, arithmetic and copies ran while one was open for 1% of the time, Pallas kernels for 7%

profile of v5, /device:TPU:31, one launch (start us, length us, event | category | flops | bytes accessed | tf_op | source)
XLA Modules:
  0.0 63.9 jit_solution(537747316227646555)
XLA Ops:
  0.0 1.4 %broadcast_in_dim.6 = f32[16,16,128]{2,1,0:T(8,128)} broadcast(f32[16,128]{1,0:T(8,128)} %param.4), dimensions={1,2} | broadcast | bytes 139264 | tf_op jit(solution)/shard_map/broadcast_in_dim | solution.py:130
  1.4 7.4 %all-to-all-start = ((f32[16,16,128]{2,1,0:T(8,128)}), f32[16,16,128]{2,1,0:T(8,128)S(1)}, u32[]{:S(2)}, u32[]{:S(2)}) async-start(f32[16,16,128]{2,1,0:T(8,128)} %broadcast_in_dim.6), calls=%async_computation | async-start | bytes 262144 | tf_op jit(solution)/shard_map/all_to_all | solution.py:133
  9.4 0.7 %compare_select_fusion.plan = s32[1,1,128]{2,1,0:T(1,128)S(1)} fusion(s32[1,1,128]{2,1,0:T(1,128)} %param.6, s32[]{:T(128)} %bitcast.2), kind=kLoop, calls=%fused_computation | loop fusion | flops 256 | bytes 1028 | tf_op jit(solution)/shard_map/jit(_where)/select_n | solution.py:132
  10.1 2.4 %all-to-all-done.x_ref = f32[16,16,128]{2,1,0:T(8,128)S(1)} async-done(((f32[16,16,128]{2,1,0:T(8,128)}), f32[16,16,128]{2,1,0:T(8,128)S(1)}, u32[]{:S(2)}, u32[]{:S(2)}) %all-to-all-start) | async-done | bytes 131104 | tf_op jit(solution)/shard_map/all_to_all | solution.py:133
  12.5 5.8 %row_terms.1 = f32[16,16,128]{2,1,0:T(8,128)} custom-call(s32[1,1,128]{2,1,0:T(1,128)S(1)} %compare_select_fusion.plan, s32[1,1]{1,0:T(1,128)} %copy.5.count_ref, f32[16,16,128]{2,1,0:T(8,128)S(1)} %all-to-all-done.x_ref, f32[128,128,128]{2,1,0:T(8,128)} %bitcast.3), custom_call_target="tpu_custom_call" | custom-call | flops 201326592 | bytes 8388608 | tf_op jit(solution)/shard_map/row_terms/pallas_call | solution.py:101
  18.3 8.9 %all-to-all-start.2 = ((f32[16,16,128]{2,1,0:T(8,128)}), f32[16,16,128]{2,1,0:T(8,128)S(1)}, u32[]{:S(2)}, u32[]{:S(2)}) async-start(f32[16,16,128]{2,1,0:T(8,128)} %row_terms.1), calls=%async_computation.2 | async-start | bytes 262144 | tf_op jit(solution)/shard_map/all_to_all | solution.py:136
  27.2 6.5 %collective-permute-start = (f32[16,16,128]{2,1,0:T(8,128)S(1)}, f32[16,16,128]{2,1,0:T(8,128)S(1)}, u32[]{:S(2)}, u32[]{:S(2)}) collective-permute-start(f32[16,16,128]{2,1,0:T(8,128)S(1)} %all-to-all-done.x_ref), channel_id=1, source_target_pairs={{32,0},{160,1},{96,2},{128,3},{0,4},{208,5},{64,6},{224,7},{48,8},... | collective-permute-start | bytes 393224 | tf_op jit(solution)/shard_map/ppermute | solution.py:134
  33.7 4.3 %collective-permute-done.x_ref = f32[16,16,128]{2,1,0:T(8,128)S(1)} collective-permute-done((f32[16,16,128]{2,1,0:T(8,128)S(1)}, f32[16,16,128]{2,1,0:T(8,128)S(1)}, u32[]{:S(2)}, u32[]{:S(2)}) %collective-permute-start) | collective-permute-done | bytes 131104 | tf_op jit(solution)/shard_map/ppermute | solution.py:134
  38.0 4.4 %col_terms.1 = f32[16,16,128]{2,1,0:T(8,128)} custom-call(s32[1,1,128]{2,1,0:T(1,128)S(1)} %compare_select_fusion.plan, s32[1,1]{1,0:T(1,128)} %copy.5.count_ref, f32[16,16,128]{2,1,0:T(8,128)S(1)} %collective-permute-done.x_ref, f32[128,128,128]{2,1,0:T(8,128)} %bitcast.4), custom_call_target="tpu_custom_call" | custom-call | flops 201326592 | bytes 8388608 | tf_op jit(solution)/shard_map/col_terms/pallas_call | solution.py:101
  42.4 0.0 all-to-all-done.2
  42.5 11.0 %all-to-all-start.1 = ((f32[16,16,128]{2,1,0:T(8,128)}), f32[16,16,128]{2,1,0:T(8,128)S(1)}, u32[]{:S(2)}, u32[]{:S(2)}) async-start(f32[16,16,128]{2,1,0:T(8,128)} %col_terms.1), calls=%async_computation.1 | async-start | bytes 262144 | tf_op jit(solution)/shard_map/all_to_all | solution.py:138
  53.5 0.9 %collective-permute-start.1 = (f32[16,128]{1,0:T(8,128)S(1)}, f32[16,128]{1,0:T(8,128)S(1)}, u32[]{:S(2)}, u32[]{:S(2)}) collective-permute-start(f32[16,128]{1,0:T(8,128)S(1)} %reduce_sum.19), channel_id=1, source_target_pairs={{0,32},{1,160},{2,96},{3,128},{4,0},{5,208},{6,64},{7,224},{8,48},... | collective-permute-start | bytes 24584 | tf_op jit(solution)/shard_map/ppermute | solution.py:139
  54.4 2.8 %all-to-all-done.1 = f32[16,16,128]{2,1,0:T(8,128)S(1)} async-done(((f32[16,16,128]{2,1,0:T(8,128)}), f32[16,16,128]{2,1,0:T(8,128)S(1)}, u32[]{:S(2)}, u32[]{:S(2)}) %all-to-all-start.1) | async-done | bytes 131104 | tf_op jit(solution)/shard_map/all_to_all | solution.py:138
  57.2 6.1 %collective-permute-done.1 = f32[16,128]{1,0:T(8,128)S(1)} collective-permute-done((f32[16,128]{1,0:T(8,128)S(1)}, f32[16,128]{1,0:T(8,128)S(1)}, u32[]{:S(2)}, u32[]{:S(2)}) %collective-permute-start.1) | collective-permute-done | bytes 8224 | tf_op jit(solution)/shard_map/ppermute | solution.py:139
  63.3 0.6 add.3
  (2 shorter events, 0.0 us)
Async XLA Ops:
  1.4 11.1 %all-to-all-start = ((f32[16,16,128]{2,1,0:T(8,128)}), f32[16,16,128]{2,1,0:T(8,128)S(1)}, u32[]{:S(2)}, u32[]{:S(2)}) async-start(f32[16,16,128]{2,1,0:T(8,128)} %broadcast_in_dim.6), calls=%async_computation | async-start | bytes 262144 | tf_op jit(solution)/shard_map/all_to_all | solution.py:133
  18.3 24.2 %all-to-all-start.2 = ((f32[16,16,128]{2,1,0:T(8,128)}), f32[16,16,128]{2,1,0:T(8,128)S(1)}, u32[]{:S(2)}, u32[]{:S(2)}) async-start(f32[16,16,128]{2,1,0:T(8,128)} %row_terms.1), calls=%async_computation.2 | async-start | bytes 262144 | tf_op jit(solution)/shard_map/all_to_all | solution.py:136
  27.2 10.8 %collective-permute-start = (f32[16,16,128]{2,1,0:T(8,128)S(1)}, f32[16,16,128]{2,1,0:T(8,128)S(1)}, u32[]{:S(2)}, u32[]{:S(2)}) collective-permute-start(f32[16,16,128]{2,1,0:T(8,128)S(1)} %all-to-all-done.x_ref), channel_id=1, source_target_pairs={{32,0},{160,1},{96,2},{128,3},{0,4},{208,5},{64,6},{224,7},{48,8},... | collective-permute-start | bytes 393224 | tf_op jit(solution)/shard_map/ppermute | solution.py:134
  42.5 14.7 %all-to-all-start.1 = ((f32[16,16,128]{2,1,0:T(8,128)}), f32[16,16,128]{2,1,0:T(8,128)S(1)}, u32[]{:S(2)}, u32[]{:S(2)}) async-start(f32[16,16,128]{2,1,0:T(8,128)} %col_terms.1), calls=%async_computation.1 | async-start | bytes 262144 | tf_op jit(solution)/shard_map/all_to_all | solution.py:138
  53.5 9.8 %collective-permute-start.1 = (f32[16,128]{1,0:T(8,128)S(1)}, f32[16,128]{1,0:T(8,128)S(1)}, u32[]{:S(2)}, u32[]{:S(2)}) collective-permute-start(f32[16,128]{1,0:T(8,128)S(1)} %reduce_sum.19), channel_id=1, source_target_pairs={{0,32},{1,160},{2,96},{3,128},{4,0},{5,208},{6,64},{7,224},{8,48},... | collective-permute-start | bytes 24584 | tf_op jit(solution)/shard_map/ppermute | solution.py:139

commit v6 on v5

v6 whole, which is shorter than its diff:
```python
import jax
import jax.numpy as jnp
from jax import lax
from jax.experimental import pallas as pl
from jax.experimental.pallas import tpu as pltpu
from jax.sharding import PartitionSpec as P


CHUNK = 16
BY_ROWS = (((1,), (0,)), ((), ()))
BY_COLS = (((1,), (1,)), ((), ()))

TURN_IN = (4, 6, 12, 2, 0, 11, 8, 14, 5, 3, 1, 15, 13, 10, 9, 7)
TURN_OUT = (4, 2, 0, 10, 1, 6, 9, 14, 13, 3, 8, 15, 5, 7, 12, 11)


def turned(turn, r, entry):
    c = ((((r >> 1) + (entry >> 1)) & 7) << 1) | ((r ^ entry) & 1)
    step = turn[entry]
    half = (r >> 3) ^ ((step >> 1) & 1)
    i = (half << 3) | ((((r >> 1) + (step >> 2)) & 3) << 1) | (step & 1)
    return c, i


def pairs(turn, n_row, n_col):
    found = []
    for r in range(n_row):
        for entry in range(n_col):
            c, i = turned(turn, r, entry)
            found.append((r * n_col + c, i * n_col + r))
    return found


def parity(turn, i, r):
    odd = sum((entry & 1) << step for entry, step in enumerate(turn))
    step = ((((i >> 1) - (r >> 1)) & 3) << 2) | (((i ^ r) >> 3) << 1) | (i & 1)
    return ((odd >> step) ^ r) & 1


def split(value):
    high = value.astype(jnp.bfloat16)
    low = (value - high.astype(jnp.float32)).astype(jnp.bfloat16)
    return high, low


def accumulate(rows_out, plan, count_ref, tiles, acc_ref, lhs_ref, held, pos_ref, done, x_parts):
    n_tiles, vecs, _ = acc_ref.shape
    bits = n_tiles.bit_length() - 1
    n_half = n_tiles // 2
    side = lax.bitwise_and(lax.axis_index("col"), 1)
    count = count_ref[0, 0]
    groups = lax.div(count + (CHUNK - 1), CHUNK)
    pos_copy = pltpu.make_async_copy(plan, pos_ref, done.at[held.shape[0] // CHUNK])
    pos_copy.start()

    def fetch(g):
        part = pl.ds(g * CHUNK, CHUNK)
        return pltpu.make_async_copy(tiles.at[part], held.at[part], done.at[g])

    def ask(g, carry):
        fetch(g).start()
        return carry

    lax.fori_loop(0, groups, ask, 0)
    first = 0
    for x_ref in x_parts:
        for t in range(x_ref.shape[0]):
            high, low = split(x_ref[t])
            upper = jnp.concatenate([high, high], axis=1)
            lower = jnp.concatenate([low, jnp.zeros_like(low)], axis=1)
            lhs_ref[first + t] = jnp.concatenate([upper, lower], axis=0)
        first += x_ref.shape[0]
    lhs_ref[n_tiles] = jnp.zeros(lhs_ref.shape[1:], jnp.bfloat16)
    acc_ref[...] = jnp.zeros_like(acc_ref)
    pos_copy.wait()

    def group(g, carry):
        fetch(g).wait()
        for u in range(CHUNK):
            slot = g * CHUNK + u
            pos = pos_ref[0, 0, slot]
            row = lax.bitwise_and(lax.shift_right_logical(pos, bits), n_tiles - 1)
            row = lax.bitwise_xor(row, side * n_half) if rows_out else row
            col = lax.bitwise_and(pos, n_tiles - 1)
            source, target = (col, row) if rows_out else (row, col)
            source = jnp.where(pos < 0, n_tiles, source)
            rhs = jnp.concatenate(split(held[slot]), axis=1 if rows_out else 0)
            both = lax.dot_general(
                lhs_ref[source],
                rhs,
                BY_COLS if rows_out else BY_ROWS,
                preferred_element_type=jnp.float32,
            )
            acc_ref[target] += both[:vecs] + both[vecs:]
        return carry

    lax.fori_loop(0, groups, group, 0)


def rows_body(plan, count_ref, x_ref, tiles, keep_ref, send_ref, acc_ref, *rest):
    accumulate(True, plan, count_ref, tiles, acc_ref, *rest, [x_ref])
    n_half = keep_ref.shape[0]
    keep_ref[...] = acc_ref[:n_half]
    send_ref[...] = acc_ref[n_half:]


def cols_body(plan, count_ref, x_ref, tiles, out_ref, *rest):
    accumulate(False, plan, count_ref, tiles, out_ref, *rest, [x_ref])


def product(rows_out, plan, count, x_parts, tiles):
    _, vecs, width = x_parts[0].shape
    n_tiles = sum(x.shape[0] for x in x_parts)
    anywhere = pl.BlockSpec(memory_space=pl.ANY)
    smem = pl.BlockSpec(memory_space=pltpu.SMEM)
    vmem = pl.BlockSpec(memory_space=pltpu.VMEM)
    whole, half = (n_tiles, vecs, width), (n_tiles // 2, vecs, width)
    out = jax.ShapeDtypeStruct(half if rows_out else whole, jnp.float32)
    acc = [pltpu.VMEM(whole, jnp.float32)] if rows_out else []
    return pl.pallas_call(
        rows_body if rows_out else cols_body,
        out_shape=(out, out) if rows_out else out,
        in_specs=[anywhere, smem, *[vmem] * len(x_parts), anywhere],
        out_specs=(vmem, vmem) if rows_out else vmem,
        scratch_shapes=[
            *acc,
            pltpu.VMEM((n_tiles + 1, 2 * vecs, 2 * width), jnp.bfloat16),
            pltpu.VMEM(tiles.shape, tiles.dtype),
            pltpu.SMEM(plan.shape, plan.dtype),
            pltpu.SemaphoreType.DMA((tiles.shape[0] // CHUNK + 1,)),
        ],
        compiler_params=pltpu.CompilerParams(vmem_limit_bytes=53 << 20),
        cost_estimate=pl.CostEstimate(
            flops=6 * vecs * tiles.size, bytes_accessed=4 * tiles.size, transcendentals=0
        ),
        name="row_terms" if rows_out else "col_terms",
    )(plan, count, *x_parts, tiles)


def local(vectors, tile_blocks, coords, counts):
    n_row = lax.axis_size("row")
    n_col = lax.axis_size("col")
    max_slots = tile_blocks.shape[2]
    vecs, tile = vectors.shape
    axes = ("row", "col")
    n_half = n_row // 2
    in_pairs = pairs(TURN_IN, n_row, n_col)
    out_pairs = pairs(TURN_OUT, n_row, n_col)
    swap = [(c, c ^ 1) for c in range(n_col)]
    tiles = tile_blocks.reshape(max_slots, tile, tile)
    spread = jnp.broadcast_to(vectors[None], (n_row, vecs, tile))
    slots = jnp.arange(max_slots, dtype=jnp.int32)
    plan = jnp.where(slots < counts[:, :, None], coords, -1)
    side = parity(TURN_OUT, lax.axis_index("row"), lax.axis_index("col"))
    x_col = lax.all_to_all(spread, "row", 0, 0, tiled=True)
    x_row = lax.ppermute(x_col, axes, [(b, a) for a, b in in_pairs])
    keep, send = product(True, plan, counts, [x_col], tiles)
    got = lax.ppermute(send, "col", swap)
    moved = lax.ppermute(keep + got, axes, out_pairs)
    col_terms = product(False, plan, counts, [x_row], tiles)
    base = side * n_half
    mine = lax.dynamic_slice_in_dim(col_terms, base, n_half, 0) + moved
    both = lax.dynamic_update_slice_in_dim(col_terms, mine, base, 0)
    col_parts = lax.all_to_all(both, "row", 0, 0, tiled=True)
    return jnp.sum(col_parts, axis=0)


def solution(mesh):
    return jax.shard_map(
        local,
        mesh=mesh,
        in_specs=(
            P(None, ("col", "row")),
            P("row", "col", None, None, None),
            P("row", "col", None),
            P("row", "col"),
        ),
        out_specs=P(None, ("col", "row")),
        check_vma=False,
    )
```

time: 64.3 us -> 56.3 us (0.88)
  the two profiles are of different devices: /device:TPU:31 before, /device:TPU:1 now
where the time goes in v6:
time: 56.3 us; the launch traced here: 56 us
  blocking collectives  18.1 us (32%)
  starting transfers between devices  15.9 us (28%)
  waiting for transfers between devices  11.3 us (20%)
  Pallas kernels  7.38 us (13%)
  local copies, waits for them, and re-layouts  1.35 us (2%)
  other arithmetic  1.3 us (2%)
  between operations  0.71 us (1%)
    all_to_all x1, blocking collectives, local(): col_parts = lax.all_to_all(both, 'row', 0, 0, tiled=True)  18.1 us
    all_to_all x1, starting transfers between devices, local(): x_col = lax.all_to_all(spread, 'row', 0, 0, tiled=True)  8.44 us
    pallas_call x2, Pallas kernels, product(): pl.pallas_call(rows_body if rows_out else cols_body, out_shape=(out, out)...  7.38 us
    ppermute x1, starting transfers between devices, local(): x_row = lax.ppermute(x_col, axes, [(b, a) for a, b in in_pairs])  7.01 us
    all_to_all x1, waiting for transfers between devices, local(): x_col = lax.all_to_all(spread, 'row', 0, 0, tiled=True)  6.3 us
    ppermute x1, waiting for transfers between devices, local(): got = lax.ppermute(send, 'col', swap)  2.87 us
    ppermute x1, waiting for transfers between devices, local(): moved = lax.ppermute(keep + got, axes, out_pairs)  2.11 us
    broadcast_in_dim x1, local copies, waits for them, and re-layouts, local(): spread = jnp.broadcast_to(vectors[None], (n_row, vecs, tile))  1.35 us
  transfers between devices with their start and end apart: 4, of which 3 were waited for; matrix products, arithmetic and copies ran while one was open for 1% of the time, Pallas kernels for 13%

profile of v6, /device:TPU:1, one launch (start us, length us, event | category | flops | bytes accessed | tf_op | source)
XLA Modules:
  0.0 56.0 jit_solution(3800926520925298012)
XLA Ops:
  0.0 1.3 %broadcast_in_dim.6 = f32[16,16,128]{2,1,0:T(8,128)} broadcast(f32[16,128]{1,0:T(8,128)} %param.4), dimensions={1,2} | broadcast | bytes 139264 | tf_op jit(solution)/shard_map/broadcast_in_dim | solution.py:151
  1.3 8.4 %all-to-all-start = ((f32[16,16,128]{2,1,0:T(8,128)}), f32[16,16,128]{2,1,0:T(8,128)S(1)}, u32[]{:S(2)}, u32[]{:S(2)}) async-start(f32[16,16,128]{2,1,0:T(8,128)} %broadcast_in_dim.6), calls=%async_computation | async-start | bytes 262144 | tf_op jit(solution)/shard_map/all_to_all | solution.py:155
  10.4 0.7 %compare_select_fusion.plan = s32[1,1,128]{2,1,0:T(1,128)S(1)} fusion(s32[1,1,128]{2,1,0:T(1,128)} %param.6, s32[]{:T(128)} %bitcast.2), kind=kLoop, calls=%fused_computation.1 | loop fusion | flops 256 | bytes 1028 | tf_op jit(solution)/shard_map/jit(_where)/select_n | solution.py:153
  11.1 6.3 %all-to-all-done.x_ref = f32[16,16,128]{2,1,0:T(8,128)S(1)} async-done(((f32[16,16,128]{2,1,0:T(8,128)}), f32[16,16,128]{2,1,0:T(8,128)S(1)}, u32[]{:S(2)}, u32[]{:S(2)}) %all-to-all-start) | async-done | bytes 131104 | tf_op jit(solution)/shard_map/all_to_all | solution.py:155
  17.4 7.0 %collective-permute-start = (f32[16,16,128]{2,1,0:T(8,128)S(1)}, f32[16,16,128]{2,1,0:T(8,128)S(1)}, u32[]{:S(2)}, u32[]{:S(2)}) collective-permute-start(f32[16,16,128]{2,1,0:T(8,128)S(1)} %all-to-all-done.x_ref), channel_id=1, source_target_pairs={{32,0},{160,1},{96,2},{128,3},{0,4},{208,5},{64,6},{224,7},{48,8},... | collective-permute-start | bytes 393224 | tf_op jit(solution)/shard_map/ppermute | solution.py:156
  24.4 4.2 %row_terms.1 = (f32[8,16,128]{2,1,0:T(8,128)S(1)}, f32[8,16,128]{2,1,0:T(8,128)S(1)}) custom-call(s32[1,1,128]{2,1,0:T(1,128)S(1)} %compare_select_fusion.plan, s32[1,1]{1,0:T(1,128)} %copy.6.count_ref, f32[16,16,128]{2,1,0:T(8,128)S(1)} %all-to-all-done.x_ref, f32[128,128,128]{2,1,0:T(8,128)} %bitcast.3), custom_call_target="tpu_custom_call" | custom-call | flops 201326592 | bytes 8388608 | tf_op jit(solution)/shard_map/row_terms/pallas_call | solution.py:120
  28.6 0.3 collective-permute-start.1
  28.9 2.9 %collective-permute-done.1 = f32[8,16,128]{2,1,0:T(8,128)S(1)} collective-permute-done((f32[8,16,128]{2,1,0:T(8,128)S(1)}, f32[8,16,128]{2,1,0:T(8,128)S(1)}, u32[]{:S(2)}, u32[]{:S(2)}) %collective-permute-start.1) | collective-permute-done | bytes 65568 | tf_op jit(solution)/shard_map/ppermute | solution.py:158
  31.8 0.1 collective-permute-start.2
  31.9 0.0 collective-permute-done.x_ref
  31.9 3.2 %col_terms.1 = f32[16,16,128]{2,1,0:T(8,128)S(1)} custom-call(s32[1,1,128]{2,1,0:T(1,128)S(1)} %compare_select_fusion.plan, s32[1,1]{1,0:T(1,128)} %copy.6.count_ref, f32[16,16,128]{2,1,0:T(8,128)S(1)} %collective-permute-done.x_ref, f32[128,128,128]{2,1,0:T(8,128)} %bitcast.4), custom_call_target="tpu_custom_call" | custom-call | flops 201326592 | bytes 8388608 | tf_op jit(solution)/shard_map/col_terms/pallas_call | solution.py:120
  35.1 2.1 %collective-permute-done.2 = f32[8,16,128]{2,1,0:T(8,128)S(1)} collective-permute-done((f32[8,16,128]{2,1,0:T(8,128)S(1)}, f32[8,16,128]{2,1,0:T(8,128)S(1)}, u32[]{:S(2)}, u32[]{:S(2)}) %collective-permute-start.2) | collective-permute-done | bytes 65568 | tf_op jit(solution)/shard_map/ppermute | solution.py:159
  37.3 18.1 %all_to_all.10 = f32[16,16,128]{2,1,0:T(8,128)S(1)} all-to-all(f32[16,16,128]{2,1,0:T(8,128)S(1)} %add_dynamic-update-slice_fusion), channel_id=1, replica_groups=mesh['row'=16,'col'=16] {'row'}, dimensions={0} | all-to-all | bytes 262144 | tf_op jit(solution)/shard_map/all_to_all | solution.py:164
  55.4 0.6 %reduce_sum.9 = f32[16,128]{1,0:T(8,128)} reduce(f32[16,16,128]{2,1,0:T(8,128)S(1)} %all_to_all.10, f32[]{:T(128)} %constant.24.clone.1), dimensions={0}, to_apply=%region_0.1 | reduce | flops 30720 | bytes 139268 | tf_op jit(solution)/shard_map/reduce_sum | solution.py:165
  (2 shorter events, 0.0 us)
Async XLA Ops:
  1.3 16.1 %all-to-all-start = ((f32[16,16,128]{2,1,0:T(8,128)}), f32[16,16,128]{2,1,0:T(8,128)S(1)}, u32[]{:S(2)}, u32[]{:S(2)}) async-start(f32[16,16,128]{2,1,0:T(8,128)} %broadcast_in_dim.6), calls=%async_computation | async-start | bytes 262144 | tf_op jit(solution)/shard_map/all_to_all | solution.py:155
  17.4 14.5 %collective-permute-start = (f32[16,16,128]{2,1,0:T(8,128)S(1)}, f32[16,16,128]{2,1,0:T(8,128)S(1)}, u32[]{:S(2)}, u32[]{:S(2)}) collective-permute-start(f32[16,16,128]{2,1,0:T(8,128)S(1)} %all-to-all-done.x_ref), channel_id=1, source_target_pairs={{32,0},{160,1},{96,2},{128,3},{0,4},{208,5},{64,6},{224,7},{48,8},... | collective-permute-start | bytes 393224 | tf_op jit(solution)/shard_map/ppermute | solution.py:156
  28.6 3.2 %collective-permute-start.1 = (f32[8,16,128]{2,1,0:T(8,128)S(1)}, f32[8,16,128]{2,1,0:T(8,128)S(1)}, u32[]{:S(2)}, u32[]{:S(2)}) collective-permute-start(f32[8,16,128]{2,1,0:T(8,128)S(1)} %get-tuple-element.8), channel_id=1, source_target_pairs={{0,1},{1,0},{2,3},{3,2},{4,5},{5,4},{6,7},{7,6},{8,9},{9,8},{10,11... | collective-permute-start | bytes 196616 | tf_op jit(solution)/shard_map/ppermute | solution.py:158
  31.8 5.4 %collective-permute-start.2 = (f32[8,16,128]{2,1,0:T(8,128)S(1)}, f32[8,16,128]{2,1,0:T(8,128)S(1)}, u32[]{:S(2)}, u32[]{:S(2)}) collective-permute-start(f32[8,16,128]{2,1,0:T(8,128)S(1)} %add.11), channel_id=1, source_target_pairs={{0,32},{1,128},{2,0},{3,192},{4,16},{5,160},{6,80},{7,224},{8,112}... | collective-permute-start | bytes 196616 | tf_op jit(solution)/shard_map/ppermute | solution.py:159

commit v7 on v6

--- a/solution.py
+++ b/solution.py
@@ -10,8 +10,7 @@
 BY_ROWS = (((1,), (0,)), ((), ()))
 BY_COLS = (((1,), (1,)), ((), ()))
 
-TURN_IN = (4, 6, 12, 2, 0, 11, 8, 14, 5, 3, 1, 15, 13, 10, 9, 7)
-TURN_OUT = (4, 2, 0, 10, 1, 6, 9, 14, 13, 3, 8, 15, 5, 7, 12, 11)
+TURN = (12, 11, 5, 10, 8, 14, 0, 6, 13, 3, 4, 2, 1, 15, 9, 7)
 
 
 def turned(turn, r, entry):
@@ -144,16 +143,16 @@
     vecs, tile = vectors.shape
     axes = ("row", "col")
     n_half = n_row // 2
-    in_pairs = pairs(TURN_IN, n_row, n_col)
-    out_pairs = pairs(TURN_OUT, n_row, n_col)
+    out_pairs = pairs(TURN, n_row, n_col)
+    in_pairs = [(b, a) for a, b in out_pairs]
     swap = [(c, c ^ 1) for c in range(n_col)]
     tiles = tile_blocks.reshape(max_slots, tile, tile)
     spread = jnp.broadcast_to(vectors[None], (n_row, vecs, tile))
     slots = jnp.arange(max_slots, dtype=jnp.int32)
     plan = jnp.where(slots < counts[:, :, None], coords, -1)
-    side = parity(TURN_OUT, lax.axis_index("row"), lax.axis_index("col"))
+    side = parity(TURN, lax.axis_index("row"), lax.axis_index("col"))
     x_col = lax.all_to_all(spread, "row", 0, 0, tiled=True)
-    x_row = lax.ppermute(x_col, axes, [(b, a) for a, b in in_pairs])
+    x_row = lax.ppermute(x_col, axes, in_pairs)
     keep, send = product(True, plan, counts, [x_col], tiles)
     got = lax.ppermute(send, "col", swap)
     moved = lax.ppermute(keep + got, axes, out_pairs)

time: 56.3 us -> 56.5 us (level)
  no operation moved by 1% of the time
where the time goes in v7:
time: 56.5 us; the launch traced here: 56.2 us
  blocking collectives  18.2 us (32%)
  starting transfers between devices  15.4 us (27%)
  waiting for transfers between devices  11.8 us (21%)
  Pallas kernels  7.38 us (13%)
  local copies, waits for them, and re-layouts  1.35 us (2%)
  other arithmetic  1.3 us (2%)
  between operations  0.71 us (1%)
    all_to_all x1, blocking collectives, local(): col_parts = lax.all_to_all(both, 'row', 0, 0, tiled=True)  18.2 us
    all_to_all x1, starting transfers between devices, local(): x_col = lax.all_to_all(spread, 'row', 0, 0, tiled=True)  8.44 us
    pallas_call x2, Pallas kernels, product(): pl.pallas_call(rows_body if rows_out else cols_body, out_shape=(out, out)...  7.38 us
    ppermute x1, starting transfers between devices, local(): x_row = lax.ppermute(x_col, axes, in_pairs)  6.56 us
    all_to_all x1, waiting for transfers between devices, local(): x_col = lax.all_to_all(spread, 'row', 0, 0, tiled=True)  6.3 us
    ppermute x1, waiting for transfers between devices, local(): got = lax.ppermute(send, 'col', swap)  2.87 us
    ppermute x1, waiting for transfers between devices, local(): moved = lax.ppermute(keep + got, axes, out_pairs)  2.66 us
    broadcast_in_dim x1, local copies, waits for them, and re-layouts, local(): spread = jnp.broadcast_to(vectors[None], (n_row, vecs, tile))  1.35 us
  transfers between devices with their start and end apart: 4, of which 3 were waited for; matrix products, arithmetic and copies ran while one was open for 1% of the time, Pallas kernels for 13%

profile of v7, /device:TPU:1, one launch (start us, length us, event | category | flops | bytes accessed | tf_op | source)
XLA Modules:
  0.0 56.2 jit_solution(8173148172115320444)
XLA Ops:
  0.0 1.3 %broadcast_in_dim.6 = f32[16,16,128]{2,1,0:T(8,128)} broadcast(f32[16,128]{1,0:T(8,128)} %param.4), dimensions={1,2} | broadcast | bytes 139264 | tf_op jit(solution)/shard_map/broadcast_in_dim | solution.py:150
  1.3 8.4 %all-to-all-start = ((f32[16,16,128]{2,1,0:T(8,128)}), f32[16,16,128]{2,1,0:T(8,128)S(1)}, u32[]{:S(2)}, u32[]{:S(2)}) async-start(f32[16,16,128]{2,1,0:T(8,128)} %broadcast_in_dim.6), calls=%async_computation | async-start | bytes 262144 | tf_op jit(solution)/shard_map/all_to_all | solution.py:154
  10.4 0.7 %compare_select_fusion.plan = s32[1,1,128]{2,1,0:T(1,128)S(1)} fusion(s32[1,1,128]{2,1,0:T(1,128)} %param.6, s32[]{:T(128)} %bitcast.2), kind=kLoop, calls=%fused_computation.1 | loop fusion | flops 256 | bytes 1028 | tf_op jit(solution)/shard_map/jit(_where)/select_n | solution.py:152
  11.1 6.3 %all-to-all-done.x_ref = f32[16,16,128]{2,1,0:T(8,128)S(1)} async-done(((f32[16,16,128]{2,1,0:T(8,128)}), f32[16,16,128]{2,1,0:T(8,128)S(1)}, u32[]{:S(2)}, u32[]{:S(2)}) %all-to-all-start) | async-done | bytes 131104 | tf_op jit(solution)/shard_map/all_to_all | solution.py:154
  17.4 6.6 %collective-permute-start = (f32[16,16,128]{2,1,0:T(8,128)S(1)}, f32[16,16,128]{2,1,0:T(8,128)S(1)}, u32[]{:S(2)}, u32[]{:S(2)}) collective-permute-start(f32[16,16,128]{2,1,0:T(8,128)S(1)} %all-to-all-done.x_ref), channel_id=1, source_target_pairs={{96,0},{208,1},{48,2},{192,3},{64,4},{224,5},{0,6},{160,7},{112,8}... | collective-permute-start | bytes 393224 | tf_op jit(solution)/shard_map/ppermute | solution.py:155
  24.0 4.2 %row_terms.1 = (f32[8,16,128]{2,1,0:T(8,128)S(1)}, f32[8,16,128]{2,1,0:T(8,128)S(1)}) custom-call(s32[1,1,128]{2,1,0:T(1,128)S(1)} %compare_select_fusion.plan, s32[1,1]{1,0:T(1,128)} %copy.6.count_ref, f32[16,16,128]{2,1,0:T(8,128)S(1)} %all-to-all-done.x_ref, f32[128,128,128]{2,1,0:T(8,128)} %bitcast.3), custom_call_target="tpu_custom_call" | custom-call | flops 201326592 | bytes 8388608 | tf_op jit(solution)/shard_map/row_terms/pallas_call | solution.py:119
  28.2 0.3 collective-permute-start.1
  28.5 2.9 %collective-permute-done.1 = f32[8,16,128]{2,1,0:T(8,128)S(1)} collective-permute-done((f32[8,16,128]{2,1,0:T(8,128)S(1)}, f32[8,16,128]{2,1,0:T(8,128)S(1)}, u32[]{:S(2)}, u32[]{:S(2)}) %collective-permute-start.1) | collective-permute-done | bytes 65568 | tf_op jit(solution)/shard_map/ppermute | solution.py:157
  31.4 0.1 collective-permute-start.2
  31.5 0.0 collective-permute-done.x_ref
  31.5 3.2 %col_terms.1 = f32[16,16,128]{2,1,0:T(8,128)S(1)} custom-call(s32[1,1,128]{2,1,0:T(1,128)S(1)} %compare_select_fusion.plan, s32[1,1]{1,0:T(1,128)} %copy.6.count_ref, f32[16,16,128]{2,1,0:T(8,128)S(1)} %collective-permute-done.x_ref, f32[128,128,128]{2,1,0:T(8,128)} %bitcast.4), custom_call_target="tpu_custom_call" | custom-call | flops 201326592 | bytes 8388608 | tf_op jit(solution)/shard_map/col_terms/pallas_call | solution.py:119
  34.7 2.7 %collective-permute-done.2 = f32[8,16,128]{2,1,0:T(8,128)S(1)} collective-permute-done((f32[8,16,128]{2,1,0:T(8,128)S(1)}, f32[8,16,128]{2,1,0:T(8,128)S(1)}, u32[]{:S(2)}, u32[]{:S(2)}) %collective-permute-start.2) | collective-permute-done | bytes 65568 | tf_op jit(solution)/shard_map/ppermute | solution.py:158
  37.4 18.2 %all_to_all.10 = f32[16,16,128]{2,1,0:T(8,128)S(1)} all-to-all(f32[16,16,128]{2,1,0:T(8,128)S(1)} %add_dynamic-update-slice_fusion), channel_id=1, replica_groups=mesh['row'=16,'col'=16] {'row'}, dimensions={0} | all-to-all | bytes 262144 | tf_op jit(solution)/shard_map/all_to_all | solution.py:163
  55.6 0.6 %reduce_sum.9 = f32[16,128]{1,0:T(8,128)} reduce(f32[16,16,128]{2,1,0:T(8,128)S(1)} %all_to_all.10, f32[]{:T(128)} %constant.24.clone.1), dimensions={0}, to_apply=%region_0.1 | reduce | flops 30720 | bytes 139268 | tf_op jit(solution)/shard_map/reduce_sum | solution.py:164
  (2 shorter events, 0.0 us)
Async XLA Ops:
  1.3 16.1 %all-to-all-start = ((f32[16,16,128]{2,1,0:T(8,128)}), f32[16,16,128]{2,1,0:T(8,128)S(1)}, u32[]{:S(2)}, u32[]{:S(2)}) async-start(f32[16,16,128]{2,1,0:T(8,128)} %broadcast_in_dim.6), calls=%async_computation | async-start | bytes 262144 | tf_op jit(solution)/shard_map/all_to_all | solution.py:154
  17.4 14.1 %collective-permute-start = (f32[16,16,128]{2,1,0:T(8,128)S(1)}, f32[16,16,128]{2,1,0:T(8,128)S(1)}, u32[]{:S(2)}, u32[]{:S(2)}) collective-permute-start(f32[16,16,128]{2,1,0:T(8,128)S(1)} %all-to-all-done.x_ref), channel_id=1, source_target_pairs={{96,0},{208,1},{48,2},{192,3},{64,4},{224,5},{0,6},{160,7},{112,8}... | collective-permute-start | bytes 393224 | tf_op jit(solution)/shard_map/ppermute | solution.py:155
  28.2 3.2 %collective-permute-start.1 = (f32[8,16,128]{2,1,0:T(8,128)S(1)}, f32[8,16,128]{2,1,0:T(8,128)S(1)}, u32[]{:S(2)}, u32[]{:S(2)}) collective-permute-start(f32[8,16,128]{2,1,0:T(8,128)S(1)} %get-tuple-element.8), channel_id=1, source_target_pairs={{0,1},{1,0},{2,3},{3,2},{4,5},{5,4},{6,7},{7,6},{8,9},{9,8},{10,11... | collective-permute-start | bytes 196616 | tf_op jit(solution)/shard_map/ppermute | solution.py:157
  31.4 6.0 %collective-permute-start.2 = (f32[8,16,128]{2,1,0:T(8,128)S(1)}, f32[8,16,128]{2,1,0:T(8,128)S(1)}, u32[]{:S(2)}, u32[]{:S(2)}) collective-permute-start(f32[8,16,128]{2,1,0:T(8,128)S(1)} %add.11), channel_id=1, source_target_pairs={{0,96},{1,208},{2,48},{3,192},{4,64},{5,224},{6,0},{7,160},{8,112}... | collective-permute-start | bytes 196616 | tf_op jit(solution)/shard_map/ppermute | solution.py:158
